TPU v7x, 32 devices: a whole 2x2x4 slice. The times are simulated.
32 devices in a mesh: rep: 2 (over core), width: 4 (over y, x), hid: 4 (over z).
Axes of the slice: x: 2, y: 2, z: 4, core: 2. Of those that a mesh axis runs over, the one named last changes fastest.
Arguments:
- tokens: float32 [128, 5120], P(('rep', 'hid'), 'width'), may hold values from -6 to 6
- cotangent: float32 [128, 5120], P(('rep', 'hid'), 'width'), may hold values from -6 to 6
- w_gate: float32 [5120, 6912], P('width', 'hid'), may hold values from -0.078125 to 0.078125
- w_up: float32 [5120, 6912], P('width', 'hid'), may hold values from -0.078125 to 0.078125
- w_down: float32 [6912, 5120], P('hid', 'width'), may hold values from -0.078125 to 0.078125
Outputs:
- output: float32 [128, 5120], P(('rep', 'hid'), 'width')
- grad_tokens: float32 [128, 5120], P(('rep', 'hid'), 'width')
- grad_gate: float32 [4, 2, 640, 6912], P('width', 'rep', None, 'hid')
- grad_up: float32 [4, 2, 640, 6912], P('width', 'rep', None, 'hid')
- grad_down: float32 [4, 2, 864, 5120], P('hid', 'rep', None, 'width')
All inputs are finite; a program needn't handle non-finite values.
Results may differ from a plain program's by a relative error of at most 0.00016.
Values sent between devices are 32-bit elements; how exact they have to be, the bound alone decides.
No kernel may reach another device: no remote copies, remote signals or barrier semaphores. Data moves between devices by JAX's collectives and lax.ppermute only.
A program may use at most 128 MiB of HBM per device.

v0:
```python
import functools

import jax
import jax.numpy as jnp
from jax import lax
from jax.experimental import pallas as pl
from jax.experimental.pallas import tpu as pltpu
from jax.sharding import PartitionSpec as P


BF = jnp.bfloat16
F32 = jnp.float32
MIB = 1 << 20
TILE = 256
VMEM = pl.BlockSpec(memory_space=pltpu.VMEM)
SMEM = pl.BlockSpec(memory_space=pltpu.SMEM)
HBM = pl.BlockSpec(memory_space=pltpu.HBM)
KEPT = pltpu.VMEM
PREPARE_LIMIT = 14


def near(value):
    return pltpu.with_memory_space_constraint(value, pltpu.VMEM)


def split(value):
    high = value.astype(BF)
    low = (value - high.astype(F32)).astype(BF)
    return high, low


def mm(left, right, dims):
    return lax.dot_general(left, right, (dims, ((), ())), preferred_element_type=F32)


def product(both, w_high, w_low, dims):
    rows = both.shape[0] // 2
    wide = mm(both, w_high, dims)
    return wide[:rows] + wide[rows:] + mm(both[:rows], w_low, dims)


def tiles(extent):
    return [(at, min(TILE, extent - at)) for at in range(0, extent, TILE)]


def call(body, out_shape, args, in_specs, scratch, flops, nbytes, limit):
    return pl.pallas_call(
        body,
        out_shape=out_shape,
        in_specs=in_specs,
        out_specs=[VMEM] * len(out_shape),
        scratch_shapes=list(scratch),
        compiler_params=pltpu.CompilerParams(vmem_limit_bytes=limit * MIB),
        cost_estimate=pl.CostEstimate(flops=flops, bytes_accessed=nbytes, transcendentals=0),
    )(*args)


def shape_of(shape, dtype=F32):
    return jax.ShapeDtypeStruct(shape, dtype)


def with_bit(places, mask):
    return [p for p in places if p & mask], [p for p in places if not p & mask]


def prepare_kernel(count, scal, *refs):
    weights, outs = refs[:count], refs[count : 3 * count]
    buffers, sems = refs[3 * count : 4 * count], refs[4 * count]
    hidden = buffers[0].shape[0]
    work = []
    for i in range(count):
        for c, (at, size) in enumerate(tiles(hidden)):
            start = pl.multiple_of(scal[0] * hidden + at, 8)
            copy = pltpu.make_async_copy(
                weights[i].at[pl.ds(start, size), :], buffers[i].at[pl.ds(at, size), :], sems.at[i, c]
            )
            copy.start()
            work.append((copy, i, at, size))
    for copy, i, at, size in work:
        copy.wait()
        high, low = split(buffers[i][at : at + size, :])
        outs[2 * i][at : at + size, :] = high
        outs[2 * i + 1][at : at + size, :] = low


def prepare(scal, weights, hidden):
    depth = weights[0].shape[1]
    count = len(weights)
    return call(
        functools.partial(prepare_kernel, count),
        [KEPT((hidden, depth), BF)] * (2 * count),
        [scal] + [pltpu.with_memory_space_constraint(w, pltpu.HBM) for w in weights],
        [SMEM] + [HBM] * count,
        [pltpu.VMEM((hidden, depth), F32)] * count + [pltpu.SemaphoreType.DMA((count, len(tiles(hidden))))],
        6 * hidden * depth * count,
        8 * hidden * depth * count,
        PREPARE_LIMIT,
    )


def forward_kernel(n, block, count, scal, *refs):
    own, far = refs[:n], refs[n : 2 * n]
    weights = refs[2 * n : 2 * n + 2 * count]
    send, keep, stack, rows_ref, part_ref = refs[2 * n + 2 * count :]
    replica, me = scal[0], scal[1]
    for source, which in ((own, replica), (far, 1 - replica)):
        for s in range(n):
            at = pl.multiple_of((which * n + s) * block, block)
            rows_ref[pl.ds(at, block), :] = source[s][...]
    both = jnp.concatenate(split(rows_ref[...]), axis=0)
    half = stack.shape[1]
    stack[...] = both if half == both.shape[1] else jnp.where(replica == 0, both[:, :half], both[:, half:])
    outs = list(zip((send, keep), with_bit(list(range(n)), 1)))
    for i in range(count):
        part_ref[...] = product(both, weights[2 * i][...], weights[2 * i + 1][...], ((1,), (1,)))
        for ref, chosen in outs:
            for place, label in enumerate(chosen):
                for k in range(2):
                    source = pl.multiple_of((k * n + (label ^ me)) * block, block)
                    at = (2 * place + k) * block
                    ref[i, at : at + block, :] = part_ref[pl.ds(source, block), :]


def forward(scal, own, far, weights, hidden, kept_width):
    n, (block, depth) = len(own), own[0].shape
    rows = 2 * n * block
    count = len(weights) // 2
    return call(
        functools.partial(forward_kernel, n, block, count),
        [shape_of((count, rows // 2, hidden))] * 2 + [shape_of((2 * rows, kept_width), BF)],
        [scal, *own, *far, *weights],
        [SMEM] + [VMEM] * (2 * n + 2 * count),
        [pltpu.VMEM((rows, depth), F32), pltpu.VMEM((rows, hidden), F32)],
        6 * rows * depth * hidden * count,
        4 * count * depth * hidden,
        10,
    )


def load_labels(refs, labels, ref_out, block, n, me, channel):
    for ref, group in zip(refs, labels):
        for place, label in enumerate(group):
            for k in range(2):
                at = pl.multiple_of((k * n + (label ^ me)) * block, block)
                source = (2 * place + k) * block
                ref_out[pl.ds(at, block), :] = ref[channel, source : source + block, :]


def store_owners(part, keep, send, first):
    half = part.shape[0] // 2
    keep[...] = jnp.where(first, part[:half], part[half:])
    send[...] = jnp.where(first, part[half:], part[:half])


def activate_kernel(labels, n, block, scal, *refs):
    parts = refs[: len(labels)]
    w_high, w_low, keep, send, turned, c_gate, c_up, gate_ref, up_ref = refs[len(labels) :]
    replica, me = scal[0], scal[1]
    load_labels(parts, labels, gate_ref, block, n, me, 0)
    load_labels(parts, labels, up_ref, block, n, me, 1)
    gate, up = gate_ref[...], up_ref[...]
    logistic = 1.0 / (1.0 + jnp.exp(-gate))
    swish = gate * logistic
    hid = swish * up
    both = jnp.concatenate(split(hid), axis=0)
    store_owners(product(both, w_high[...], w_low[...], ((1,), (0,))), keep, send, replica == 0)
    c_up[...] = swish
    c_gate[...] = up * logistic * (1.0 + gate * (1.0 - logistic))
    turned[...] = jnp.concatenate(split(hid.T), axis=1)


def backward_kernel(labels, n, block, scal, *refs):
    parts = refs[: len(labels)]
    c_gate, c_up, g_high, g_low, u_high, u_low, keep, send, turned, grad_ref = refs[len(labels) :]
    replica, me = scal[0], scal[1]
    load_labels(parts, labels, grad_ref, block, n, me, 0)
    grad = grad_ref[...]
    gg = grad * c_gate[...]
    ug = grad * c_up[...]
    g_both = jnp.concatenate(split(gg), axis=0)
    u_both = jnp.concatenate(split(ug), axis=0)
    dims = ((1,), (0,))
    part = product(g_both, g_high[...], g_low[...], dims) + product(u_both, u_high[...], u_low[...], dims)
    store_owners(part, keep, send, replica == 0)
    turned[...] = jnp.concatenate([gg.T, ug.T], axis=1)


def outer(left, right):
    rows = right.shape[0] // 2
    high, low = right[:rows], right[rows:]
    return mm(jnp.concatenate([left, left[:, :rows]], 1), jnp.concatenate([high, high, low], 0), ((1,), (0,)))


def down_kernel(left, right, out):
    out[...] = outer(left[...], right[...])


def wide_kernel(scal, own, far, right, g_out, u_out):
    value = jnp.where(pl.program_id(0) == scal[0], own[...], far[...])
    rows = value.shape[1] // 2
    for out, part in ((g_out, value[:, :rows]), (u_out, value[:, rows:])):
        out[...] = outer(jnp.concatenate(split(part), axis=1), right[...])


def add_kernel(group, picks, keep, got, *outs):
    for out, chosen in zip(outs, picks):
        for at, i in enumerate(chosen):
            rows = slice(i * group, (i + 1) * group)
            out[:, at * group : (at + 1) * group, :] = keep[:, rows, :] + got[:, rows, :]


def add_groups(keep, got, group, picks):
    count, _, width = keep.shape
    return call(
        functools.partial(add_kernel, group, picks),
        [shape_of((count, len(chosen) * group, width)) for chosen in picks],
        [keep, got],
        [VMEM] * 2,
        [],
        keep.size,
        12 * keep.size,
        6,
    )


def total_kernel(*refs):
    *parts, out = refs
    value = parts[0][...]
    for part in parts[1:]:
        value = value + part[...]
    out[...] = value


def total_of(parts):
    shape = parts[0].shape
    size = parts[0].size
    return call(
        total_kernel, [shape_of(shape)], parts, [VMEM] * len(parts), [], size * len(parts), 4 * size * len(parts), 4
    )[0]


def shards(n_rep, n_width, n_hid, tokens, cotangent, w_gate, w_up, w_down):
    block, depth = tokens.shape
    full = w_gate.shape[1]
    hidden, half_width = full // n_rep, depth // n_rep
    assert n_rep == 2 and n_width == n_hid
    n = n_hid
    levels = n.bit_length() - 1
    rows = n_rep * n * block
    group = n_rep * block
    replica, place = lax.axis_index("rep"), lax.axis_index("width")
    turned = sum(((place >> i) & 1) << (levels - 1 - i) for i in range(levels))
    me = jnp.where(replica == 0, place, turned)
    scal = jnp.stack([replica, me]).astype(jnp.int32)

    def shift(value, s):
        return lax.ppermute(value, "hid", [(i, i ^ s) for i in range(n)])

    def swap(value):
        return lax.ppermute(value, "rep", [(0, 1), (1, 0)])

    def hop(value, level):
        masks = (1 << level, 1 << (levels - 1 - level))
        pairs = [(r * n + i, r * n + (i ^ masks[r])) for r in range(2) for i in range(n)]
        return lax.ppermute(value, ("rep", "width"), pairs)

    def gather(value):
        own = [value] + [shift(value, s) for s in range(1, n)]
        return own, [swap(v) for v in own]

    def reduce_over_width(send, keep):
        labels = list(range(n))
        for level in range(levels):
            labels = with_bit(labels, 1 << level)[1]
            got = hop(send, level)
            if level + 1 < levels:
                picks = [[labels.index(p) for p in some] for some in with_bit(labels, 2 << level)]
                send, keep = add_groups(keep, got, group, picks)
        held = [([0], add_groups(keep, got, group, [[0]])[0])]
        for level in reversed(range(levels)):
            held = held + [([p ^ (1 << level) for p in some], hop(value, level)) for some, value in held]
        return [value for _, value in held], [some for some, _ in held]

    def to_owner(keep, send):
        got = swap(send)
        blocks = add_groups(keep[None], got[None], block, [[s] for s in range(n)])
        blocks = [b[0] for b in blocks]
        return total_of([blocks[0]] + [shift(blocks[s], s) for s in range(1, n)])

    x_own, x_far = gather(tokens)
    y_own, y_far = gather(cotangent)
    wgu = prepare(scal, [w_gate.T, w_up.T], hidden)
    wd = prepare(scal, [w_down], hidden)
    wgu, wd = [near(w) for w in wgu], [near(w) for w in wd]
    *outs, x_half = forward(scal, x_own, x_far, wgu, hidden, half_width)
    gu_parts, labels = reduce_over_width(*outs)
    *outs, y_both = forward(scal, y_own, y_far, wd, hidden, depth)
    gh_parts, _ = reduce_over_width(*outs)

    narrow = [shape_of((n * block, depth))] * 2
    keep, send, hid_turned, c_gate, c_up = call(
        functools.partial(activate_kernel, labels, n, block),
        narrow + [shape_of((hidden, 2 * rows), BF)] + [shape_of((rows, hidden))] * 2,
        [scal, *gu_parts, *wd],
        [SMEM] + [VMEM] * (len(gu_parts) + 2),
        [pltpu.VMEM((rows, hidden), F32)] * 2,
        6 * rows * hidden * depth,
        4 * hidden * depth,
        8,
    )
    output = to_owner(keep, send)

    tile = depth // 2 if depth % TILE == 0 else depth
    grad_down = pl.pallas_call(
        down_kernel,
        out_shape=shape_of((hidden, depth)),
        in_specs=[
            pl.BlockSpec((hidden, 2 * rows), lambda i: (0, 0)),
            pl.BlockSpec((2 * rows, tile), lambda i: (0, i)),
        ],
        out_specs=pl.BlockSpec((hidden, tile), lambda i: (0, i)),
        grid=(depth // tile,),
        compiler_params=pltpu.CompilerParams(vmem_limit_bytes=14 * MIB),
        cost_estimate=pl.CostEstimate(flops=6 * rows * hidden * depth, bytes_accessed=4 * hidden * depth, transcendentals=0),
        name="down",
    )(hid_turned, y_both)

    keep, send, grads = call(
        functools.partial(backward_kernel, labels, n, block),
        narrow + [shape_of((hidden, 2 * rows))],
        [scal, *gh_parts, c_gate, c_up, *wgu],
        [SMEM] + [VMEM] * (len(gh_parts) + 6),
        [pltpu.VMEM((rows, hidden), F32)],
        12 * rows * hidden * depth,
        8 * hidden * depth,
        8,
    )
    far = swap(grads)
    grad_tokens = to_owner(keep, send)

    chunks = 2 if hidden % 16 == 0 else 1
    lines = hidden // chunks
    side = pl.BlockSpec((lines, 2 * rows), lambda i, j: (j, 0))
    grad_gate, grad_up = pl.pallas_call(
        wide_kernel,
        out_shape=[shape_of((full, half_width))] * 2,
        in_specs=[SMEM, side, side, pl.BlockSpec((2 * rows, half_width), lambda i, j: (0, 0))],
        out_specs=[pl.BlockSpec((lines, half_width), lambda i, j: (i * chunks + j, 0))] * 2,
        grid=(n_rep, chunks),
        compiler_params=pltpu.CompilerParams(vmem_limit_bytes=14 * MIB),
        cost_estimate=pl.CostEstimate(
            flops=12 * rows * half_width * full, bytes_accessed=8 * half_width * full, transcendentals=0
        ),
        name="wide",
    )(scal, grads, far, x_half)
    return (
        output,
        grad_tokens,
        grad_gate.T.reshape(1, 1, half_width, full),
        grad_up.T.reshape(1, 1, half_width, full),
        grad_down.reshape(1, 1, hidden, depth),
    )


def solution(mesh):
    sizes = [mesh.shape[a] for a in ("rep", "width", "hid")]
    return jax.shard_map(
        functools.partial(shards, *sizes),
        mesh=mesh,
        in_specs=(
            P(("rep", "hid"), "width"),
            P(("rep", "hid"), "width"),
            P("width", "hid"),
            P("width", "hid"),
            P("hid", "width"),
        ),
        out_specs=(
            P(("rep", "hid"), "width"),
            P(("rep", "hid"), "width"),
            P("width", "rep", None, "hid"),
            P("width", "rep", None, "hid"),
            P("hid", "rep", None, "width"),
        ),
        check_vma=False,
    )
```

profile of v0, /device:TPU:0, one launch (start us, length us, event | category | flops | bytes accessed | tf_op | source)
XLA Modules:
  0.0 94.0 jit_solution(4264363662049914056)
XLA Ops:
  0.6 3.1 %collective-permute-start = (f32[16,1280]{1,0:T(8,128)}, f32[16,1280]{1,0:T(8,128)S(1)}, u32[]{:S(2)}, u32[]{:S(2)}) collective-permute-start(f32[16,1280]{1,0:T(8,128)} %refs_0_.3), channel_id=1, source_target_pairs={{0,1},{1,0},{2,3},{3,2},{4,5},{5,4},{6,7},{7,6},{8,9},{9,8},{10,11... | collective-permute-start | bytes 245768 | tf_op jit(solution)/shard_map/ppermute | solution.py:257
  3.7 2.6 %collective-permute-start.1 = (f32[16,1280]{1,0:T(8,128)}, f32[16,1280]{1,0:T(8,128)S(1)}, u32[]{:S(2)}, u32[]{:S(2)}) collective-permute-start(f32[16,1280]{1,0:T(8,128)} %refs_0_.3), channel_id=1, source_target_pairs={{0,2},{1,3},{2,0},{3,1},{4,6},{5,7},{6,4},{7,5},{8,10},{9,11},{10,... | collective-permute-start | bytes 245768 | tf_op jit(solution)/shard_map/ppermute | solution.py:257
  6.9 6.3 %collective-permute-done.1.refs_2_ = f32[16,1280]{1,0:T(8,128)S(1)} collective-permute-done((f32[16,1280]{1,0:T(8,128)}, f32[16,1280]{1,0:T(8,128)S(1)}, u32[]{:S(2)}, u32[]{:S(2)}) %collective-permute-start.1) | collective-permute-done | bytes 81952 | tf_op jit(solution)/shard_map/ppermute | solution.py:257
  13.8 4.3 %shard_map.92 = (bf16[864,1280]{1,0:T(8,128)(2,1)S(1)}, bf16[864,1280]{1,0:T(8,128)(2,1)S(1)}, bf16[864,1280]{1,0:T(8,128)(2,1)S(1)}, bf16[864,1280]{1,0:T(8,128)(2,1)S(1)}) custom-call(s32[2]{0:T(128)S(1)} %pad_add_fusion.scal, f32[1728,1280]{1,0:T(8,128)} %bitcast.35, f32[1728,1280]{1,0:T(8,128)} %bitcast.36), custom_call_target="tpu_custom_call" | custom-call | flops 13271040 | bytes 17694720 | tf_op jit(solution)/shard_map/pallas_call | solution.py:47
  18.1 3.4 %shard_map.93 = (f32[2,64,864]{2,1,0:T(8,128)S(1)}, f32[2,64,864]{2,1,0:T(8,128)S(1)}, bf16[256,640]{1,0:T(8,128)(2,1)S(1)}) custom-call(s32[2]{0:T(128)S(1)} %pad_add_fusion.scal, f32[16,1280]{1,0:T(8,128)S(1)} %copy-done, f32[16,1280]{1,0:T(8,128)S(1)} %collective-permute-done.refs_1_, f32[16,1280]{1,0:T(8,128)S(1)} %collective-permute-done.1.refs_2_, ...), custom_call_target="tpu_custom_call" | custom-call | flops 1698693120 | bytes 8847360 | tf_op jit(solution)/shard_map/pallas_call | solution.py:47
  21.5 1.6 %collective-permute-start.7 = (f32[2,64,864]{2,1,0:T(8,128)S(1)}, f32[2,64,864]{2,1,0:T(8,128)S(1)}, u32[]{:S(2)}, u32[]{:S(2)}) collective-permute-start(f32[2,64,864]{2,1,0:T(8,128)S(1)} %get-tuple-element.44), channel_id=1, source_target_pairs={{0,4},{4,0},{8,12},{12,8},{16,24},{20,28},{24,16},{28,20},{1,5},{5... | collective-permute-start | bytes 1327112 | tf_op jit(solution)/shard_map/ppermute | solution.py:265
  24.0 2.1 %collective-permute-start.17 = (f32[16,1280]{1,0:T(8,128)S(1)}, f32[16,1280]{1,0:T(8,128)S(1)}, u32[]{:S(2)}, u32[]{:S(2)}) collective-permute-start(f32[16,1280]{1,0:T(8,128)S(1)} %copy-done.1), channel_id=1, source_target_pairs={{0,2},{1,3},{2,0},{3,1},{4,6},{5,7},{6,4},{7,5},{8,10},{9,11},{10,... | collective-permute-start | bytes 245768 | tf_op jit(solution)/shard_map/ppermute | solution.py:257
  27.5 2.6 %collective-permute-done.7.got = f32[2,64,864]{2,1,0:T(8,128)S(1)} collective-permute-done((f32[2,64,864]{2,1,0:T(8,128)S(1)}, f32[2,64,864]{2,1,0:T(8,128)S(1)}, u32[]{:S(2)}, u32[]{:S(2)}) %collective-permute-start.7) | collective-permute-done | bytes 442400 | tf_op jit(solution)/shard_map/ppermute | solution.py:265
  30.1 1.6 %collective-permute-start.8 = (f32[2,32,864]{2,1,0:T(8,128)S(1)}, f32[2,32,864]{2,1,0:T(8,128)S(1)}, u32[]{:S(2)}, u32[]{:S(2)}) collective-permute-start(f32[2,32,864]{2,1,0:T(8,128)S(1)} %get-tuple-element.46), channel_id=1, source_target_pairs={{0,8},{4,12},{8,0},{12,4},{16,20},{20,16},{24,28},{28,24},{1,9},{5... | collective-permute-start | bytes 663560 | tf_op jit(solution)/shard_map/ppermute | solution.py:265
  34.1 2.9 %shard_map.96 = (bf16[864,1280]{1,0:T(8,128)(2,1)S(1)}, bf16[864,1280]{1,0:T(8,128)(2,1)S(1)}) custom-call(s32[2]{0:T(128)S(1)} %pad_add_fusion.scal, f32[1728,1280]{1,0:T(8,128)} %refs_0_.4), custom_call_target="tpu_custom_call" | custom-call | flops 6635520 | bytes 8847360 | tf_op jit(solution)/shard_map/pallas_call | solution.py:47
  37.1 2.1 %shard_map.100 = (f32[1,64,864]{2,1,0:T(8,128)S(1)}, f32[1,64,864]{2,1,0:T(8,128)S(1)}, bf16[256,1280]{1,0:T(8,128)(2,1)S(1)}) custom-call(s32[2]{0:T(128)S(1)} %pad_add_fusion.scal, f32[16,1280]{1,0:T(8,128)S(1)} %copy-done.1, f32[16,1280]{1,0:T(8,128)S(1)} %collective-permute-done.16.refs_1_, f32[16,1280]{1,0:T(8,128)S(1)} %collective-permute-done.17.refs_2_, ...), custom_call_target="tpu_custom_call" | custom-call | flops 849346560 | bytes 4423680 | tf_op jit(solution)/shard_map/pallas_call | solution.py:47
  41.4 5.8 %collective-permute-done.23.got = f32[1,64,864]{2,1,0:T(8,128)S(1)} collective-permute-done((f32[1,64,864]{2,1,0:T(8,128)S(1)}, f32[1,64,864]{2,1,0:T(8,128)S(1)}, u32[]{:S(2)}, u32[]{:S(2)}) %collective-permute-start.23) | collective-permute-done | bytes 221216 | tf_op jit(solution)/shard_map/ppermute | solution.py:265
  50.2 3.1 %collective-permute-done.24.got = f32[1,32,864]{2,1,0:T(8,128)S(1)} collective-permute-done((f32[1,32,864]{2,1,0:T(8,128)S(1)}, f32[1,32,864]{2,1,0:T(8,128)S(1)}, u32[]{:S(2)}, u32[]{:S(2)}) %collective-permute-start.24) | collective-permute-done | bytes 110624 | tf_op jit(solution)/shard_map/ppermute | solution.py:265
  55.6 3.3 %collective-permute-done.25.refs_1_ = f32[1,32,864]{2,1,0:T(8,128)S(1)} collective-permute-done((f32[1,32,864]{2,1,0:T(8,128)S(1)}, f32[1,32,864]{2,1,0:T(8,128)S(1)}, u32[]{:S(2)}, u32[]{:S(2)}) %collective-permute-start.25) | collective-permute-done | bytes 110624 | tf_op jit(solution)/shard_map/ppermute | solution.py:265
  59.3 1.9 %shard_map.97 = (f32[64,1280]{1,0:T(8,128)S(1)}, f32[64,1280]{1,0:T(8,128)S(1)}, bf16[864,256]{1,0:T(8,128)(2,1)S(1)}, f32[128,864]{1,0:T(8,128)S(1)}, f32[128,864]{1,0:T(8,128)S(1)}) custom-call(s32[2]{0:T(128)S(1)} %pad_add_fusion.scal, f32[2,32,864]{2,1,0:T(8,128)S(1)} %shard_map.95.refs_0_, f32[2,32,864]{2,1,0:T(8,128)S(1)} %collective-permute-done.9.refs_1_, ...), custom_call_target="tpu_custom_call" | custom-call | flops 849346560 | bytes 4423680 | tf_op jit(solution)/shard_map/pallas_call | solution.py:47
  61.2 2.5 %collective-permute-done.27.refs_3_ = f32[1,32,864]{2,1,0:T(8,128)S(1)} collective-permute-done((f32[1,32,864]{2,1,0:T(8,128)S(1)}, f32[1,32,864]{2,1,0:T(8,128)S(1)}, u32[]{:S(2)}, u32[]{:S(2)}) %collective-permute-start.27) | collective-permute-done | bytes 110624 | tf_op jit(solution)/shard_map/ppermute | solution.py:265
  63.7 2.8 %shard_map.103 = (f32[64,1280]{1,0:T(8,128)S(1)}, f32[64,1280]{1,0:T(8,128)S(1)}, f32[864,256]{1,0:T(8,128)S(1)}) custom-call(s32[2]{0:T(128)S(1)} %pad_add_fusion.scal, f32[1,32,864]{2,1,0:T(8,128)S(1)} %shard_map.102.refs_0_, f32[1,32,864]{2,1,0:T(8,128)S(1)} %collective-permute-done.25.refs_1_, f32[1,32,864]{2,1,0:T(8,128)S(1)} %collective-permute-done.26.refs_2_, ...), custom_call_target="tpu_custom_call" | custom-call | flops 1698693120 | bytes 8847360 | tf_op jit(solution)/shard_map/pallas_call | solution.py:47
  67.1 2.3 %collective-permute-done.12 = f32[64,1280]{1,0:T(8,128)S(1)} collective-permute-done((f32[64,1280]{1,0:T(8,128)S(1)}, f32[64,1280]{1,0:T(8,128)S(1)}, u32[]{:S(2)}, u32[]{:S(2)}) %collective-permute-start.12) | collective-permute-done | bytes 327712 | tf_op jit(solution)/shard_map/ppermute | solution.py:260
  69.5 2.0 %collective-permute-start.13 = (f32[16,1280]{1,0:T(8,128)S(1)}, f32[16,1280]{1,0:T(8,128)S(1)}, u32[]{:S(2)}, u32[]{:S(2)}) collective-permute-start(f32[16,1280]{1,0:T(8,128)S(1)} %bitcast.34), channel_id=1, source_target_pairs={{0,1},{1,0},{2,3},{3,2},{4,5},{5,4},{6,7},{7,6},{8,9},{9,8},{10,11... | collective-permute-start | bytes 245768 | tf_op jit(solution)/shard_map/ppermute | solution.py:257
  75.1 2.7 %collective-permute-start.30 = (f32[16,1280]{1,0:T(8,128)S(1)}, f32[16,1280]{1,0:T(8,128)S(1)}, u32[]{:S(2)}, u32[]{:S(2)}) collective-permute-start(f32[16,1280]{1,0:T(8,128)S(1)} %bitcast.31), channel_id=1, source_target_pairs={{0,2},{1,3},{2,0},{3,1},{4,6},{5,7},{6,4},{7,5},{8,10},{9,11},{10,... | collective-permute-start | bytes 245768 | tf_op jit(solution)/shard_map/ppermute | solution.py:257
  77.8 3.3 %collective-permute-done.14.refs_2_ = f32[16,1280]{1,0:T(8,128)S(1)} collective-permute-done((f32[16,1280]{1,0:T(8,128)S(1)}, f32[16,1280]{1,0:T(8,128)S(1)}, u32[]{:S(2)}, u32[]{:S(2)}) %collective-permute-start.14) | collective-permute-done | bytes 81952 | tf_op jit(solution)/shard_map/ppermute | solution.py:257
  81.0 2.7 %collective-permute-start.31 = (f32[16,1280]{1,0:T(8,128)S(1)}, f32[16,1280]{1,0:T(8,128)S(1)}, u32[]{:S(2)}, u32[]{:S(2)}) collective-permute-start(f32[16,1280]{1,0:T(8,128)S(1)} %bitcast.30), channel_id=1, source_target_pairs={{0,3},{1,2},{2,1},{3,0},{4,7},{5,6},{6,5},{7,4},{8,11},{9,10},{10,... | collective-permute-start | bytes 245768 | tf_op jit(solution)/shard_map/ppermute | solution.py:257
  83.7 3.0 %down.1 = f32[864,1280]{1,0:T(8,128)} custom-call(bf16[864,256]{1,0:T(8,128)(2,1)S(1)} %get-tuple-element.71.left, bf16[256,1280]{1,0:T(8,128)(2,1)S(1)} %get-tuple-element.72.right), custom_call_target="tpu_custom_call" | custom-call | flops 849346560 | bytes 4423680 | tf_op jit(solution)/shard_map/down/pallas_call | solution.py:314
  88.6 5.3 %wide.1 = (f32[1728,640]{1,0:T(8,128)}, f32[1728,640]{1,0:T(8,128)}) custom-call(s32[2]{0:T(128)S(1)} %pad_add_fusion.scal, f32[864,256]{1,0:T(8,128)S(1)} %get-tuple-element.67.own, f32[864,256]{1,0:T(8,128)S(1)} %collective-permute-done.32.far, bf16[256,640]{1,0:T(8,128)(2,1)S(1)} %get-tuple-element.68.right), custom_call_target="tpu_custom_call" | custom-call | flops 1698693120 | bytes 8847360 | tf_op jit(solution)/shard_map/wide/pallas_call | solution.py:344
  (63 shorter events, 19.9 us)
Async XLA Ops:
  0.6 5.8 %collective-permute-start = (f32[16,1280]{1,0:T(8,128)}, f32[16,1280]{1,0:T(8,128)S(1)}, u32[]{:S(2)}, u32[]{:S(2)}) collective-permute-start(f32[16,1280]{1,0:T(8,128)} %refs_0_.3), channel_id=1, source_target_pairs={{0,1},{1,0},{2,3},{3,2},{4,5},{5,4},{6,7},{7,6},{8,9},{9,8},{10,11... | collective-permute-start | bytes 245768 | tf_op jit(solution)/shard_map/ppermute | solution.py:257
  3.7 9.4 %collective-permute-start.1 = (f32[16,1280]{1,0:T(8,128)}, f32[16,1280]{1,0:T(8,128)S(1)}, u32[]{:S(2)}, u32[]{:S(2)}) collective-permute-start(f32[16,1280]{1,0:T(8,128)} %refs_0_.3), channel_id=1, source_target_pairs={{0,2},{1,3},{2,0},{3,1},{4,6},{5,7},{6,4},{7,5},{8,10},{9,11},{10,... | collective-permute-start | bytes 245768 | tf_op jit(solution)/shard_map/ppermute | solution.py:257
  6.3 6.8 %collective-permute-start.2 = (f32[16,1280]{1,0:T(8,128)}, f32[16,1280]{1,0:T(8,128)S(1)}, u32[]{:S(2)}, u32[]{:S(2)}) collective-permute-start(f32[16,1280]{1,0:T(8,128)} %refs_0_.3), channel_id=1, source_target_pairs={{0,3},{1,2},{2,1},{3,0},{4,7},{5,6},{6,5},{7,4},{8,11},{9,10},{10,... | collective-permute-start | bytes 245768 | tf_op jit(solution)/shard_map/ppermute | solution.py:257
  6.3 11.7 %collective-permute-start.3 = (f32[16,1280]{1,0:T(8,128)}, f32[16,1280]{1,0:T(8,128)S(1)}, u32[]{:S(2)}, u32[]{:S(2)}) collective-permute-start(f32[16,1280]{1,0:T(8,128)} %refs_0_.3), channel_id=1, source_target_pairs={{0,16},{16,0},{1,17},{17,1},{2,18},{18,2},{3,19},{19,3},{4,20},{20... | collective-permute-start | bytes 245768 | tf_op jit(solution)/shard_map/ppermute | solution.py:260
  6.4 11.7 %collective-permute-start.4 = (f32[16,1280]{1,0:T(8,128)S(1)}, f32[16,1280]{1,0:T(8,128)S(1)}, u32[]{:S(2)}, u32[]{:S(2)}) collective-permute-start(f32[16,1280]{1,0:T(8,128)S(1)} %collective-permute-done.refs_1_), channel_id=1, source_target_pairs={{0,16},{16,0},{1,17},{17,1},{2,18},{18,2},{3,19},{19,3},{4,20},{20... | collective-permute-start | bytes 245768 | tf_op jit(solution)/shard_map/ppermute | solution.py:260
  21.5 8.5 %collective-permute-start.7 = (f32[2,64,864]{2,1,0:T(8,128)S(1)}, f32[2,64,864]{2,1,0:T(8,128)S(1)}, u32[]{:S(2)}, u32[]{:S(2)}) collective-permute-start(f32[2,64,864]{2,1,0:T(8,128)S(1)} %get-tuple-element.44), channel_id=1, source_target_pairs={{0,4},{4,0},{8,12},{12,8},{16,24},{20,28},{24,16},{28,20},{1,5},{5... | collective-permute-start | bytes 1327112 | tf_op jit(solution)/shard_map/ppermute | solution.py:265
  23.1 8.6 %collective-permute-start.16 = (f32[16,1280]{1,0:T(8,128)S(1)}, f32[16,1280]{1,0:T(8,128)S(1)}, u32[]{:S(2)}, u32[]{:S(2)}) collective-permute-start(f32[16,1280]{1,0:T(8,128)S(1)} %copy-done.1), channel_id=1, source_target_pairs={{0,1},{1,0},{2,3},{3,2},{4,5},{5,4},{6,7},{7,6},{8,9},{9,8},{10,11... | collective-permute-start | bytes 245768 | tf_op jit(solution)/shard_map/ppermute | solution.py:257
  24.0 9.5 %collective-permute-start.17 = (f32[16,1280]{1,0:T(8,128)S(1)}, f32[16,1280]{1,0:T(8,128)S(1)}, u32[]{:S(2)}, u32[]{:S(2)}) collective-permute-start(f32[16,1280]{1,0:T(8,128)S(1)} %copy-done.1), channel_id=1, source_target_pairs={{0,2},{1,3},{2,0},{3,1},{4,6},{5,7},{6,4},{7,5},{8,10},{9,11},{10,... | collective-permute-start | bytes 245768 | tf_op jit(solution)/shard_map/ppermute | solution.py:257
  26.1 7.4 %collective-permute-start.18 = (f32[16,1280]{1,0:T(8,128)S(1)}, f32[16,1280]{1,0:T(8,128)S(1)}, u32[]{:S(2)}, u32[]{:S(2)}) collective-permute-start(f32[16,1280]{1,0:T(8,128)S(1)} %copy-done.1), channel_id=1, source_target_pairs={{0,3},{1,2},{2,1},{3,0},{4,7},{5,6},{6,5},{7,4},{8,11},{9,10},{10,... | collective-permute-start | bytes 245768 | tf_op jit(solution)/shard_map/ppermute | solution.py:257
  30.1 9.9 %collective-permute-start.8 = (f32[2,32,864]{2,1,0:T(8,128)S(1)}, f32[2,32,864]{2,1,0:T(8,128)S(1)}, u32[]{:S(2)}, u32[]{:S(2)}) collective-permute-start(f32[2,32,864]{2,1,0:T(8,128)S(1)} %get-tuple-element.46), channel_id=1, source_target_pairs={{0,8},{4,12},{8,0},{12,4},{16,20},{20,16},{24,28},{28,24},{1,9},{5... | collective-permute-start | bytes 663560 | tf_op jit(solution)/shard_map/ppermute | solution.py:265
  39.2 8.0 %collective-permute-start.23 = (f32[1,64,864]{2,1,0:T(8,128)S(1)}, f32[1,64,864]{2,1,0:T(8,128)S(1)}, u32[]{:S(2)}, u32[]{:S(2)}) collective-permute-start(f32[1,64,864]{2,1,0:T(8,128)S(1)} %get-tuple-element.56), channel_id=1, source_target_pairs={{0,4},{4,0},{8,12},{12,8},{16,24},{20,28},{24,16},{28,20},{1,5},{5... | collective-permute-start | bytes 663560 | tf_op jit(solution)/shard_map/ppermute | solution.py:265
  40.0 9.4 %collective-permute-start.9 = (f32[2,32,864]{2,1,0:T(8,128)S(1)}, f32[2,32,864]{2,1,0:T(8,128)S(1)}, u32[]{:S(2)}, u32[]{:S(2)}) collective-permute-start(f32[2,32,864]{2,1,0:T(8,128)S(1)} %shard_map.95.refs_0_), channel_id=1, source_target_pairs={{0,8},{4,12},{8,0},{12,4},{16,20},{20,16},{24,28},{28,24},{1,9},{5... | collective-permute-start | bytes 663560 | tf_op jit(solution)/shard_map/ppermute | solution.py:265
  47.2 6.1 %collective-permute-start.24 = (f32[1,32,864]{2,1,0:T(8,128)S(1)}, f32[1,32,864]{2,1,0:T(8,128)S(1)}, u32[]{:S(2)}, u32[]{:S(2)}) collective-permute-start(f32[1,32,864]{2,1,0:T(8,128)S(1)} %get-tuple-element.58), channel_id=1, source_target_pairs={{0,8},{4,12},{8,0},{12,4},{16,20},{20,16},{24,28},{28,24},{1,9},{5... | collective-permute-start | bytes 331784 | tf_op jit(solution)/shard_map/ppermute | solution.py:265
  48.1 11.2 %collective-permute-start.10 = (f32[2,32,864]{2,1,0:T(8,128)S(1)}, f32[2,32,864]{2,1,0:T(8,128)S(1)}, u32[]{:S(2)}, u32[]{:S(2)}) collective-permute-start(f32[2,32,864]{2,1,0:T(8,128)S(1)} %shard_map.95.refs_0_), channel_id=1, source_target_pairs={{0,4},{4,0},{8,12},{12,8},{16,24},{20,28},{24,16},{28,20},{1,5},{5... | collective-permute-start | bytes 663560 | tf_op jit(solution)/shard_map/ppermute | solution.py:265
  49.5 9.9 %collective-permute-start.11 = (f32[2,32,864]{2,1,0:T(8,128)S(1)}, f32[2,32,864]{2,1,0:T(8,128)S(1)}, u32[]{:S(2)}, u32[]{:S(2)}) collective-permute-start(f32[2,32,864]{2,1,0:T(8,128)S(1)} %collective-permute-done.9.refs_1_), channel_id=1, source_target_pairs={{0,4},{4,0},{8,12},{12,8},{16,24},{20,28},{24,16},{28,20},{1,5},{5... | collective-permute-start | bytes 663560 | tf_op jit(solution)/shard_map/ppermute | solution.py:265
  54.2 7.0 %collective-permute-start.26 = (f32[1,32,864]{2,1,0:T(8,128)S(1)}, f32[1,32,864]{2,1,0:T(8,128)S(1)}, u32[]{:S(2)}, u32[]{:S(2)}) collective-permute-start(f32[1,32,864]{2,1,0:T(8,128)S(1)} %shard_map.102.refs_0_), channel_id=1, source_target_pairs={{0,4},{4,0},{8,12},{12,8},{16,24},{20,28},{24,16},{28,20},{1,5},{5... | collective-permute-start | bytes 331784 | tf_op jit(solution)/shard_map/ppermute | solution.py:265
  66.5 22.1 %collective-permute-start.32 = (f32[864,256]{1,0:T(8,128)S(1)}, f32[864,256]{1,0:T(8,128)S(1)}, u32[]{:S(2)}, u32[]{:S(2)}) collective-permute-start(f32[864,256]{1,0:T(8,128)S(1)} %get-tuple-element.67.own), channel_id=1, source_target_pairs={{0,16},{16,0},{1,17},{17,1},{2,18},{18,2},{3,19},{19,3},{4,20},{20... | collective-permute-start | bytes 2654216 | tf_op jit(solution)/shard_map/ppermute | solution.py:260
  67.0 6.9 %collective-permute-start.28 = (f32[64,1280]{1,0:T(8,128)S(1)}, f32[64,1280]{1,0:T(8,128)S(1)}, u32[]{:S(2)}, u32[]{:S(2)}) collective-permute-start(f32[64,1280]{1,0:T(8,128)S(1)} %get-tuple-element.62), channel_id=1, source_target_pairs={{0,16},{16,0},{1,17},{17,1},{2,18},{18,2},{3,19},{19,3},{4,20},{20... | collective-permute-start | bytes 983048 | tf_op jit(solution)/shard_map/ppermute | solution.py:260
  69.5 5.6 %collective-permute-start.13 = (f32[16,1280]{1,0:T(8,128)S(1)}, f32[16,1280]{1,0:T(8,128)S(1)}, u32[]{:S(2)}, u32[]{:S(2)}) collective-permute-start(f32[16,1280]{1,0:T(8,128)S(1)} %bitcast.34), channel_id=1, source_target_pairs={{0,1},{1,0},{2,3},{3,2},{4,5},{5,4},{6,7},{7,6},{8,9},{9,8},{10,11... | collective-permute-start | bytes 245768 | tf_op jit(solution)/shard_map/ppermute | solution.py:257
  71.5 9.5 %collective-permute-start.14 = (f32[16,1280]{1,0:T(8,128)S(1)}, f32[16,1280]{1,0:T(8,128)S(1)}, u32[]{:S(2)}, u32[]{:S(2)}) collective-permute-start(f32[16,1280]{1,0:T(8,128)S(1)} %bitcast.32), channel_id=1, source_target_pairs={{0,2},{1,3},{2,0},{3,1},{4,6},{5,7},{6,4},{7,5},{8,10},{9,11},{10,... | collective-permute-start | bytes 245768 | tf_op jit(solution)/shard_map/ppermute | solution.py:257
  72.5 14.2 %collective-permute-start.15 = (f32[16,1280]{1,0:T(8,128)S(1)}, f32[16,1280]{1,0:T(8,128)S(1)}, u32[]{:S(2)}, u32[]{:S(2)}) collective-permute-start(f32[16,1280]{1,0:T(8,128)S(1)} %bitcast.29), channel_id=1, source_target_pairs={{0,3},{1,2},{2,1},{3,0},{4,7},{5,6},{6,5},{7,4},{8,11},{9,10},{10,... | collective-permute-start | bytes 245768 | tf_op jit(solution)/shard_map/ppermute | solution.py:257
  74.0 13.4 %collective-permute-start.29 = (f32[16,1280]{1,0:T(8,128)S(1)}, f32[16,1280]{1,0:T(8,128)S(1)}, u32[]{:S(2)}, u32[]{:S(2)}) collective-permute-start(f32[16,1280]{1,0:T(8,128)S(1)} %bitcast.33), channel_id=1, source_target_pairs={{0,1},{1,0},{2,3},{3,2},{4,5},{5,4},{6,7},{7,6},{8,9},{9,8},{10,11... | collective-permute-start | bytes 245768 | tf_op jit(solution)/shard_map/ppermute | solution.py:257
  75.1 12.9 %collective-permute-start.30 = (f32[16,1280]{1,0:T(8,128)S(1)}, f32[16,1280]{1,0:T(8,128)S(1)}, u32[]{:S(2)}, u32[]{:S(2)}) collective-permute-start(f32[16,1280]{1,0:T(8,128)S(1)} %bitcast.31), channel_id=1, source_target_pairs={{0,2},{1,3},{2,0},{3,1},{4,6},{5,7},{6,4},{7,5},{8,10},{9,11},{10,... | collective-permute-start | bytes 245768 | tf_op jit(solution)/shard_map/ppermute | solution.py:257
  81.0 6.9 %collective-permute-start.31 = (f32[16,1280]{1,0:T(8,128)S(1)}, f32[16,1280]{1,0:T(8,128)S(1)}, u32[]{:S(2)}, u32[]{:S(2)}) collective-permute-start(f32[16,1280]{1,0:T(8,128)S(1)} %bitcast.30), channel_id=1, source_target_pairs={{0,3},{1,2},{2,1},{3,0},{4,7},{5,6},{6,5},{7,4},{8,11},{9,10},{10,... | collective-permute-start | bytes 245768 | tf_op jit(solution)/shard_map/ppermute | solution.py:257
  (11 other events, 50.0 us)
where the time goes:
time: 94.1 us; the launch traced here: 94 us
  starting transfers between devices  34.6 us (37%)
  waiting for transfers between devices  31.2 us (33%)
  Pallas kernels  27.2 us (29%)
    ppermute x12, starting transfers between devices, shift(): return lax.ppermute(value, 'hid', [(i, i ^ s) for i in range(n)])  21 us
    pallas_call x14, Pallas kernels, call(): pl.pallas_call(body, out_shape=out_shape, in_specs=in_specs, out_specs=[V...  18.9 us
    ppermute x10, waiting for transfers between devices, hop(): return lax.ppermute(value, ('rep', 'width'), pairs)  17.3 us
    ppermute x12, waiting for transfers between devices, shift(): return lax.ppermute(value, 'hid', [(i, i ^ s) for i in range(n)])  11.6 us
    ppermute x10, starting transfers between devices, hop(): return lax.ppermute(value, ('rep', 'width'), pairs)  11 us
    pallas_call x1, Pallas kernels, shards(): pl.pallas_call(wide_kernel, out_shape=[shape_of((full, half_width))] * 2,...  5.34 us
    pallas_call x1, Pallas kernels, shards(): pl.pallas_call(down_kernel, out_shape=shape_of((hidden, depth)), in_specs...  3.01 us
    ppermute x11, starting transfers between devices, swap(): return lax.ppermute(value, 'rep', [(0, 1), (1, 0)])  2.63 us
  transfers between devices with their start and end apart: 33, of which 11 were waited for; matrix products, arithmetic and copies ran while one was open for 0% of the time, Pallas kernels for 17%

commit v1 on v0

--- a/solution.py
+++ b/solution.py
@@ -16,7 +16,7 @@
 SMEM = pl.BlockSpec(memory_space=pltpu.SMEM)
 HBM = pl.BlockSpec(memory_space=pltpu.HBM)
 KEPT = pltpu.VMEM
-PREPARE_LIMIT = 14
+PREPARE_LIMIT = 20
 
 
 def near(value):
@@ -43,12 +43,12 @@
     return [(at, min(TILE, extent - at)) for at in range(0, extent, TILE)]
 
 
-def call(body, out_shape, args, in_specs, scratch, flops, nbytes, limit):
+def call(body, out_shape, args, in_specs, scratch, flops, nbytes, limit, out_spec=VMEM):
     return pl.pallas_call(
         body,
         out_shape=out_shape,
         in_specs=in_specs,
-        out_specs=[VMEM] * len(out_shape),
+        out_specs=[out_spec] * len(out_shape),
         scratch_shapes=list(scratch),
         compiler_params=pltpu.CompilerParams(vmem_limit_bytes=limit * MIB),
         cost_estimate=pl.CostEstimate(flops=flops, bytes_accessed=nbytes, transcendentals=0),
@@ -191,15 +191,34 @@
     return mm(jnp.concatenate([left, left[:, :rows]], 1), jnp.concatenate([high, high, low], 0), ((1,), (0,)))
 
 
-def down_kernel(left, right, out):
-    out[...] = outer(left[...], right[...])
-
-
-def wide_kernel(scal, own, far, right, g_out, u_out):
-    value = jnp.where(pl.program_id(0) == scal[0], own[...], far[...])
-    rows = value.shape[1] // 2
-    for out, part in ((g_out, value[:, :rows]), (u_out, value[:, rows:])):
-        out[...] = outer(jnp.concatenate(split(part), axis=1), right[...])
+def pieces(extent):
+    cuts = [extent * i // 4 // 16 * 16 for i in range(4)] + [extent]
+    return [(at, end - at) for at, end in zip(cuts, cuts[1:])]
+
+
+def weights_kernel(scal, own, far, x_right, h_left, y_right, g_out, u_out, d_out, g_buffer, u_buffer, d_buffer, sems):
+    lines, rows = own.shape[0], own.shape[1] // 2
+    copies = []
+
+    def send(buffer, out, start, size):
+        rows_at = pl.ds(pl.multiple_of(start, 8), size)
+        copy = pltpu.make_async_copy(buffer, out.at[rows_at, :], sems.at[len(copies)])
+        copy.start()
+        copies.append(copy)
+
+    for at, size in pieces(lines):
+        piece = d_buffer.at[pl.ds(at, size), :]
+        d_buffer[at : at + size, :] = outer(h_left[at : at + size, :], y_right[...])
+        send(piece, d_out, at, size)
+    for out, buffer, first in ((g_out, g_buffer, 0), (u_out, u_buffer, rows)):
+        for k, (source, which) in enumerate(((own, scal[0]), (far, 1 - scal[0]))):
+            for at, size in pieces(lines):
+                left = jnp.concatenate(split(source[at : at + size, first : first + rows]), axis=1)
+                here = k * lines + at
+                buffer[here : here + size, :] = outer(left, x_right[...])
+                send(buffer.at[pl.ds(here, size), :], out, which * lines + at, size)
+    for copy in copies:
+        copy.wait()
 
 
 def add_kernel(group, picks, keep, got, *outs):
@@ -223,20 +242,29 @@
     )
 
 
-def total_kernel(*refs):
-    *parts, out = refs
-    value = parts[0][...]
-    for part in parts[1:]:
-        value = value + part[...]
-    out[...] = value
-
-
-def total_of(parts):
-    shape = parts[0].shape
-    size = parts[0].size
+def finish_kernel(counts, *refs):
+    parts, outs = refs[: sum(counts)], refs[sum(counts) :]
+    for out, count in zip(outs, counts):
+        value = parts[0][...]
+        for part in parts[1:count]:
+            value = value + part[...]
+        out[...] = value
+        parts = parts[count:]
+
+
+def finish(groups):
+    shape, size = groups[0][0].shape, groups[0][0].size
+    parts = [part for group in groups for part in group]
     return call(
-        total_kernel, [shape_of(shape)], parts, [VMEM] * len(parts), [], size * len(parts), 4 * size * len(parts), 4
-    )[0]
+        functools.partial(finish_kernel, [len(group) for group in groups]),
+        [shape_of(shape)] * len(groups),
+        parts,
+        [VMEM] * len(parts),
+        [],
+        size * len(parts),
+        4 * size * len(parts),
+        4,
+    )
 
 
 def shards(n_rep, n_width, n_hid, tokens, cotangent, w_gate, w_up, w_down):
@@ -265,7 +293,7 @@
         return lax.ppermute(value, ("rep", "width"), pairs)
 
     def gather(value):
-        own = [value] + [shift(value, s) for s in range(1, n)]
+        own = [value] + [shift(value, s) for s in reversed(range(1, n))][::-1]
         return own, [swap(v) for v in own]
 
     def reduce_over_width(send, keep):
@@ -284,14 +312,24 @@
     def to_owner(keep, send):
         got = swap(send)
         blocks = add_groups(keep[None], got[None], block, [[s] for s in range(n)])
-        blocks = [b[0] for b in blocks]
-        return total_of([blocks[0]] + [shift(blocks[s], s) for s in range(1, n)])
+        moved = [shift(blocks[s][0], s) for s in reversed(range(1, n))]
+        return [blocks[0][0]] + moved
+
+    def to_owner_by_hops(keep, send):
+        got = swap(send)
+        keep, got = keep[None], got[None]
+        labels = list(range(n))
+        for level in range(levels):
+            picks = [[labels.index(p) for p in some] for some in with_bit(labels, 1 << level)]
+            labels = with_bit(labels, 1 << level)[1]
+            send, keep = add_groups(keep, got, block, picks)
+            got = shift(send, 1 << level)
+        return [keep[0], got[0]]
 
     x_own, x_far = gather(tokens)
     y_own, y_far = gather(cotangent)
-    wgu = prepare(scal, [w_gate.T, w_up.T], hidden)
-    wd = prepare(scal, [w_down], hidden)
-    wgu, wd = [near(w) for w in wgu], [near(w) for w in wd]
+    prepared = [near(w) for w in prepare(scal, [w_gate.T, w_up.T, w_down], hidden)]
+    wgu, wd = prepared[:4], prepared[4:]
     *outs, x_half = forward(scal, x_own, x_far, wgu, hidden, half_width)
     gu_parts, labels = reduce_over_width(*outs)
     *outs, y_both = forward(scal, y_own, y_far, wd, hidden, depth)
@@ -308,22 +346,7 @@
         4 * hidden * depth,
         8,
     )
-    output = to_owner(keep, send)
-
-    tile = depth // 2 if depth % TILE == 0 else depth
-    grad_down = pl.pallas_call(
-        down_kernel,
-        out_shape=shape_of((hidden, depth)),
-        in_specs=[
-            pl.BlockSpec((hidden, 2 * rows), lambda i: (0, 0)),
-            pl.BlockSpec((2 * rows, tile), lambda i: (0, i)),
-        ],
-        out_specs=pl.BlockSpec((hidden, tile), lambda i: (0, i)),
-        grid=(depth // tile,),
-        compiler_params=pltpu.CompilerParams(vmem_limit_bytes=14 * MIB),
-        cost_estimate=pl.CostEstimate(flops=6 * rows * hidden * depth, bytes_accessed=4 * hidden * depth, transcendentals=0),
-        name="down",
-    )(hid_turned, y_both)
+    output_parts = to_owner_by_hops(keep, send)
 
     keep, send, grads = call(
         functools.partial(backward_kernel, labels, n, block),
@@ -336,23 +359,21 @@
         8,
     )
     far = swap(grads)
-    grad_tokens = to_owner(keep, send)
-
-    chunks = 2 if hidden % 16 == 0 else 1
-    lines = hidden // chunks
-    side = pl.BlockSpec((lines, 2 * rows), lambda i, j: (j, 0))
-    grad_gate, grad_up = pl.pallas_call(
-        wide_kernel,
-        out_shape=[shape_of((full, half_width))] * 2,
-        in_specs=[SMEM, side, side, pl.BlockSpec((2 * rows, half_width), lambda i, j: (0, 0))],
-        out_specs=[pl.BlockSpec((lines, half_width), lambda i, j: (i * chunks + j, 0))] * 2,
-        grid=(n_rep, chunks),
-        compiler_params=pltpu.CompilerParams(vmem_limit_bytes=14 * MIB),
-        cost_estimate=pl.CostEstimate(
-            flops=12 * rows * half_width * full, bytes_accessed=8 * half_width * full, transcendentals=0
-        ),
-        name="wide",
-    )(scal, grads, far, x_half)
+    token_parts = to_owner(keep, send)
+
+    shapes = [(full, half_width), (full, half_width), (hidden, depth)]
+    grad_gate, grad_up, grad_down = call(
+        weights_kernel,
+        [shape_of(shape) for shape in shapes],
+        [scal, grads, far, x_half, hid_turned, y_both],
+        [SMEM] + [VMEM] * 5,
+        [pltpu.VMEM(shape, F32) for shape in shapes] + [pltpu.SemaphoreType.DMA((20,))],
+        18 * rows * half_width * full,
+        12 * half_width * full,
+        20,
+        HBM,
+    )
+    output, grad_tokens = finish([output_parts, token_parts])
     return (
         output,
         grad_tokens,

time: 94.1 us -> 92 us (0.978)
  waiting for transfers between devices: 31.2 us -> 37.2 us
  Pallas kernels: 27.2 us -> 22.6 us
  starting transfers between devices: 34.6 us -> 31 us
    pallas_call x16 -> x14, Pallas kernels: 27.2 us -> 22.6 us  [call(): pl.pallas_call(body, out_shape=out_shape, in_specs=in_specs, out_specs=[o...]
    ppermute x12 -> x11, waiting for transfers between devices: 11.6 us -> 15.2 us  [shift(): return lax.ppermute(value, 'hid', [(i, i ^ s) for i in range(n)])]
    ppermute x12 -> x11, starting transfers between devices: 21 us -> 18.1 us  [shift(): return lax.ppermute(value, 'hid', [(i, i ^ s) for i in range(n)])]
    ppermute x10, waiting for transfers between devices: 17.3 us -> 18.8 us  [hop(): return lax.ppermute(value, ('rep', 'width'), pairs)]
  transfers between devices with their start and end apart: 33 -> 32, of which waited for: 11 -> 15; matrix products, arithmetic and copies ran while one was open for 0% -> 0% of each run, Pallas kernels for 17% -> 11%
where the time goes in v1:
time: 92 us; the launch traced here: 91.9 us
  waiting for transfers between devices  37.2 us (40%)
  starting transfers between devices  31 us (34%)
  Pallas kernels  22.6 us (25%)
  between operations  0.95 us (1%)
    pallas_call x14, Pallas kernels, call(): pl.pallas_call(body, out_shape=out_shape, in_specs=in_specs, out_specs=[o...  22.6 us
    ppermute x10, waiting for transfers between devices, hop(): return lax.ppermute(value, ('rep', 'width'), pairs)  18.8 us
    ppermute x11, starting transfers between devices, shift(): return lax.ppermute(value, 'hid', [(i, i ^ s) for i in range(n)])  18.1 us
    ppermute x11, waiting for transfers between devices, shift(): return lax.ppermute(value, 'hid', [(i, i ^ s) for i in range(n)])  15.2 us
    ppermute x10, starting transfers between devices, hop(): return lax.ppermute(value, ('rep', 'width'), pairs)  10.3 us
    ppermute x11, waiting for transfers between devices, swap(): return lax.ppermute(value, 'rep', [(0, 1), (1, 0)])  3.24 us
    ppermute x11, starting transfers between devices, swap(): return lax.ppermute(value, 'rep', [(0, 1), (1, 0)])  2.63 us
  transfers between devices with their start and end apart: 32, of which 15 were waited for; matrix products, arithmetic and copies ran while one was open for 0% of the time, Pallas kernels for 11%

profile of v1, /device:TPU:0, one launch (start us, length us, event | category | flops | bytes accessed | tf_op | source)
XLA Modules:
  0.0 91.9 jit_solution(12237884623206206985)
XLA Ops:
  0.6 3.1 %collective-permute-start = (f32[16,1280]{1,0:T(8,128)}, f32[16,1280]{1,0:T(8,128)S(1)}, u32[]{:S(2)}, u32[]{:S(2)}) collective-permute-start(f32[16,1280]{1,0:T(8,128)} %refs_0_.2), channel_id=1, source_target_pairs={{0,1},{1,0},{2,3},{3,2},{4,5},{5,4},{6,7},{7,6},{8,9},{9,8},{10,11... | collective-permute-start | bytes 245768 | tf_op jit(solution)/shard_map/ppermute | solution.py:285
  3.7 2.6 %collective-permute-start.1 = (f32[16,1280]{1,0:T(8,128)}, f32[16,1280]{1,0:T(8,128)S(1)}, u32[]{:S(2)}, u32[]{:S(2)}) collective-permute-start(f32[16,1280]{1,0:T(8,128)} %refs_0_.2), channel_id=1, source_target_pairs={{0,2},{1,3},{2,0},{3,1},{4,6},{5,7},{6,4},{7,5},{8,10},{9,11},{10,... | collective-permute-start | bytes 245768 | tf_op jit(solution)/shard_map/ppermute | solution.py:285
  6.9 6.3 %collective-permute-done.1.refs_2_ = f32[16,1280]{1,0:T(8,128)S(1)} collective-permute-done((f32[16,1280]{1,0:T(8,128)}, f32[16,1280]{1,0:T(8,128)S(1)}, u32[]{:S(2)}, u32[]{:S(2)}) %collective-permute-start.1) | collective-permute-done | bytes 81952 | tf_op jit(solution)/shard_map/ppermute | solution.py:285
  13.8 5.6 %shard_map.92 = (bf16[864,1280]{1,0:T(8,128)(2,1)S(1)}, bf16[864,1280]{1,0:T(8,128)(2,1)S(1)}, bf16[864,1280]{1,0:T(8,128)(2,1)S(1)}, bf16[864,1280]{1,0:T(8,128...) custom-call(s32[2]{0:T(128)S(1)} %pad_add_fusion.scal, f32[1728,1280]{1,0:T(8,128)} %bitcast.31, ...), custom_call_target="tpu_custom_call" | custom-call | flops 19906560 | bytes 26542080 | tf_op jit(solution)/shard_map/pallas_call | solution.py:47
  19.4 3.4 %shard_map.93 = (f32[2,64,864]{2,1,0:T(8,128)S(1)}, f32[2,64,864]{2,1,0:T(8,128)S(1)}, bf16[256,640]{1,0:T(8,128)(2,1)S(1)}) custom-call(s32[2]{0:T(128)S(1)} %pad_add_fusion.scal, f32[16,1280]{1,0:T(8,128)S(1)} %copy-done, f32[16,1280]{1,0:T(8,128)S(1)} %collective-permute-done.refs_1_, f32[16,1280]{1,0:T(8,128)S(1)} %collective-permute-done.1.refs_2_, ...), custom_call_target="tpu_custom_call" | custom-call | flops 1698693120 | bytes 8847360 | tf_op jit(solution)/shard_map/pallas_call | solution.py:47
  25.3 2.1 %collective-permute-start.16 = (f32[16,1280]{1,0:T(8,128)S(1)}, f32[16,1280]{1,0:T(8,128)S(1)}, u32[]{:S(2)}, u32[]{:S(2)}) collective-permute-start(f32[16,1280]{1,0:T(8,128)S(1)} %copy-done.1), channel_id=1, source_target_pairs={{0,2},{1,3},{2,0},{3,1},{4,6},{5,7},{6,4},{7,5},{8,10},{9,11},{10,... | collective-permute-start | bytes 245768 | tf_op jit(solution)/shard_map/ppermute | solution.py:285
  28.8 2.6 %collective-permute-done.7.got = f32[2,64,864]{2,1,0:T(8,128)S(1)} collective-permute-done((f32[2,64,864]{2,1,0:T(8,128)S(1)}, f32[2,64,864]{2,1,0:T(8,128)S(1)}, u32[]{:S(2)}, u32[]{:S(2)}) %collective-permute-start.7) | collective-permute-done | bytes 442400 | tf_op jit(solution)/shard_map/ppermute | solution.py:293
  31.4 1.6 %collective-permute-start.8 = (f32[2,32,864]{2,1,0:T(8,128)S(1)}, f32[2,32,864]{2,1,0:T(8,128)S(1)}, u32[]{:S(2)}, u32[]{:S(2)}) collective-permute-start(f32[2,32,864]{2,1,0:T(8,128)S(1)} %get-tuple-element.49), channel_id=1, source_target_pairs={{0,8},{4,12},{8,0},{12,4},{16,20},{20,16},{24,28},{28,24},{1,9},{5... | collective-permute-start | bytes 663560 | tf_op jit(solution)/shard_map/ppermute | solution.py:293
  36.3 2.1 %shard_map.99 = (f32[1,64,864]{2,1,0:T(8,128)S(1)}, f32[1,64,864]{2,1,0:T(8,128)S(1)}, bf16[256,1280]{1,0:T(8,128)(2,1)S(1)}) custom-call(s32[2]{0:T(128)S(1)} %pad_add_fusion.scal, f32[16,1280]{1,0:T(8,128)S(1)} %copy-done.1, f32[16,1280]{1,0:T(8,128)S(1)} %collective-permute-done.15.refs_1_, f32[16,1280]{1,0:T(8,128)S(1)} %collective-permute-done.16.refs_2_, ...), custom_call_target="tpu_custom_call" | custom-call | flops 849346560 | bytes 4423680 | tf_op jit(solution)/shard_map/pallas_call | solution.py:47
  40.6 6.2 %collective-permute-done.22.got = f32[1,64,864]{2,1,0:T(8,128)S(1)} collective-permute-done((f32[1,64,864]{2,1,0:T(8,128)S(1)}, f32[1,64,864]{2,1,0:T(8,128)S(1)}, u32[]{:S(2)}, u32[]{:S(2)}) %collective-permute-start.22) | collective-permute-done | bytes 221216 | tf_op jit(solution)/shard_map/ppermute | solution.py:293
  47.0 2.0 %collective-permute-start.10 = (f32[2,32,864]{2,1,0:T(8,128)S(1)}, f32[2,32,864]{2,1,0:T(8,128)S(1)}, u32[]{:S(2)}, u32[]{:S(2)}) collective-permute-start(f32[2,32,864]{2,1,0:T(8,128)S(1)} %shard_map.95.refs_0_), channel_id=1, source_target_pairs={{0,4},{4,0},{8,12},{12,8},{16,24},{20,28},{24,16},{28,20},{1,5},{5... | collective-permute-start | bytes 663560 | tf_op jit(solution)/shard_map/ppermute | solution.py:293
  49.0 3.8 %collective-permute-done.23.got = f32[1,32,864]{2,1,0:T(8,128)S(1)} collective-permute-done((f32[1,32,864]{2,1,0:T(8,128)S(1)}, f32[1,32,864]{2,1,0:T(8,128)S(1)}, u32[]{:S(2)}, u32[]{:S(2)}) %collective-permute-start.23) | collective-permute-done | bytes 110624 | tf_op jit(solution)/shard_map/ppermute | solution.py:293
  53.1 2.0 %collective-permute-start.25 = (f32[1,32,864]{2,1,0:T(8,128)S(1)}, f32[1,32,864]{2,1,0:T(8,128)S(1)}, u32[]{:S(2)}, u32[]{:S(2)}) collective-permute-start(f32[1,32,864]{2,1,0:T(8,128)S(1)} %shard_map.101.refs_0_), channel_id=1, source_target_pairs={{0,4},{4,0},{8,12},{12,8},{16,24},{20,28},{24,16},{28,20},{1,5},{5... | collective-permute-start | bytes 331784 | tf_op jit(solution)/shard_map/ppermute | solution.py:293
  55.1 3.8 %collective-permute-done.24.refs_1_ = f32[1,32,864]{2,1,0:T(8,128)S(1)} collective-permute-done((f32[1,32,864]{2,1,0:T(8,128)S(1)}, f32[1,32,864]{2,1,0:T(8,128)S(1)}, u32[]{:S(2)}, u32[]{:S(2)}) %collective-permute-start.24) | collective-permute-done | bytes 110624 | tf_op jit(solution)/shard_map/ppermute | solution.py:293
  59.4 1.9 %shard_map.96 = (f32[64,1280]{1,0:T(8,128)S(1)}, f32[64,1280]{1,0:T(8,128)S(1)}, bf16[864,256]{1,0:T(8,128)(2,1)S(1)}, f32[128,864]{1,0:T(8,128)S(1)}, f32[128,864]{1,0:T(8,128)S(1)}) custom-call(s32[2]{0:T(128)S(1)} %pad_add_fusion.scal, f32[2,32,864]{2,1,0:T(8,128)S(1)} %shard_map.95.refs_0_, f32[2,32,864]{2,1,0:T(8,128)S(1)} %collective-permute-done.9.refs_1_, ...), custom_call_target="tpu_custom_call" | custom-call | flops 849346560 | bytes 4423680 | tf_op jit(solution)/shard_map/pallas_call | solution.py:47
  61.3 2.4 %collective-permute-done.26.refs_3_ = f32[1,32,864]{2,1,0:T(8,128)S(1)} collective-permute-done((f32[1,32,864]{2,1,0:T(8,128)S(1)}, f32[1,32,864]{2,1,0:T(8,128)S(1)}, u32[]{:S(2)}, u32[]{:S(2)}) %collective-permute-start.26) | collective-permute-done | bytes 110624 | tf_op jit(solution)/shard_map/ppermute | solution.py:293
  63.7 2.8 %shard_map.102 = (f32[64,1280]{1,0:T(8,128)S(1)}, f32[64,1280]{1,0:T(8,128)S(1)}, f32[864,256]{1,0:T(8,128)S(1)}) custom-call(s32[2]{0:T(128)S(1)} %pad_add_fusion.scal, f32[1,32,864]{2,1,0:T(8,128)S(1)} %shard_map.101.refs_0_, f32[1,32,864]{2,1,0:T(8,128)S(1)} %collective-permute-done.24.refs_1_, f32[1,32,864]{2,1,0:T(8,128)S(1)} %collective-permute-done.25.refs_2_, ...), custom_call_target="tpu_custom_call" | custom-call | flops 1698693120 | bytes 8847360 | tf_op jit(solution)/shard_map/pallas_call | solution.py:47
  67.1 2.3 %collective-permute-done.12 = f32[64,1280]{1,0:T(8,128)S(1)} collective-permute-done((f32[64,1280]{1,0:T(8,128)S(1)}, f32[64,1280]{1,0:T(8,128)S(1)}, u32[]{:S(2)}, u32[]{:S(2)}) %collective-permute-start.12) | collective-permute-done | bytes 327712 | tf_op jit(solution)/shard_map/ppermute | solution.py:288
  70.6 2.6 %collective-permute-start.28 = (f32[16,1280]{1,0:T(8,128)S(1)}, f32[16,1280]{1,0:T(8,128)S(1)}, u32[]{:S(2)}, u32[]{:S(2)}) collective-permute-start(f32[16,1280]{1,0:T(8,128)S(1)} %bitcast.30), channel_id=1, source_target_pairs={{0,3},{1,2},{2,1},{3,0},{4,7},{5,6},{6,5},{7,4},{8,11},{9,10},{10,... | collective-permute-start | bytes 245768 | tf_op jit(solution)/shard_map/ppermute | solution.py:285
  73.2 1.9 %collective-permute-start.30 = (f32[16,1280]{1,0:T(8,128)S(1)}, f32[16,1280]{1,0:T(8,128)S(1)}, u32[]{:S(2)}, u32[]{:S(2)}) collective-permute-start(f32[16,1280]{1,0:T(8,128)S(1)} %bitcast.28), channel_id=1, source_target_pairs={{0,1},{1,0},{2,3},{3,2},{4,5},{5,4},{6,7},{7,6},{8,9},{9,8},{10,11... | collective-permute-start | bytes 245768 | tf_op jit(solution)/shard_map/ppermute | solution.py:285
  76.3 2.5 %collective-permute-start.14 = (f32[1,16,1280]{2,1,0:T(8,128)S(1)}, f32[1,16,1280]{2,1,0:T(8,128)S(1)}, u32[]{:S(2)}, u32[]{:S(2)}) collective-permute-start(f32[1,16,1280]{2,1,0:T(8,128)S(1)} %get-tuple-element.57), channel_id=1, source_target_pairs={{0,2},{1,3},{2,0},{3,1},{4,6},{5,7},{6,4},{7,5},{8,10},{9,11},{10,... | collective-permute-start | bytes 245768 | tf_op jit(solution)/shard_map/ppermute | solution.py:285
  79.8 3.0 %collective-permute-done.29.refs_4_ = f32[16,1280]{1,0:T(8,128)S(1)} collective-permute-done((f32[16,1280]{1,0:T(8,128)S(1)}, f32[16,1280]{1,0:T(8,128)S(1)}, u32[]{:S(2)}, u32[]{:S(2)}) %collective-permute-start.29) | collective-permute-done | bytes 81952 | tf_op jit(solution)/shard_map/ppermute | solution.py:285
  82.9 2.2 %collective-permute-done.14 = f32[1,16,1280]{2,1,0:T(8,128)S(1)} collective-permute-done((f32[1,16,1280]{2,1,0:T(8,128)S(1)}, f32[1,16,1280]{2,1,0:T(8,128)S(1)}, u32[]{:S(2)}, u32[]{:S(2)}) %collective-permute-start.14) | collective-permute-done | bytes 81952 | tf_op jit(solution)/shard_map/ppermute | solution.py:285
  85.7 6.0 %shard_map.105 = (f32[1728,640]{1,0:T(8,128)}, f32[1728,640]{1,0:T(8,128)}, f32[864,1280]{1,0:T(8,128)}) custom-call(s32[2]{0:T(128)S(1)} %pad_add_fusion.scal, f32[864,256]{1,0:T(8,128)S(1)} %get-tuple-element.72.own, f32[864,256]{1,0:T(8,128)S(1)} %collective-permute-done.31.far, bf16[256,640]{1,0:T(8,128)(2,1)S(1)} %get-tuple-element.73.x_right, ...), custom_call_target="tpu_custom_call" | custom-call | flops 2548039680 | bytes 13271040 | tf_op jit(solution)/shard_map/pallas_call | solution.py:47
  (59 shorter events, 16.3 us)
Async XLA Ops:
  3.7 9.4 %collective-permute-start.1 = (f32[16,1280]{1,0:T(8,128)}, f32[16,1280]{1,0:T(8,128)S(1)}, u32[]{:S(2)}, u32[]{:S(2)}) collective-permute-start(f32[16,1280]{1,0:T(8,128)} %refs_0_.2), channel_id=1, source_target_pairs={{0,2},{1,3},{2,0},{3,1},{4,6},{5,7},{6,4},{7,5},{8,10},{9,11},{10,... | collective-permute-start | bytes 245768 | tf_op jit(solution)/shard_map/ppermute | solution.py:285
  6.3 6.8 %collective-permute-start.2 = (f32[16,1280]{1,0:T(8,128)}, f32[16,1280]{1,0:T(8,128)S(1)}, u32[]{:S(2)}, u32[]{:S(2)}) collective-permute-start(f32[16,1280]{1,0:T(8,128)} %refs_0_.2), channel_id=1, source_target_pairs={{0,3},{1,2},{2,1},{3,0},{4,7},{5,6},{6,5},{7,4},{8,11},{9,10},{10,... | collective-permute-start | bytes 245768 | tf_op jit(solution)/shard_map/ppermute | solution.py:285
  6.3 13.0 %collective-permute-start.3 = (f32[16,1280]{1,0:T(8,128)}, f32[16,1280]{1,0:T(8,128)S(1)}, u32[]{:S(2)}, u32[]{:S(2)}) collective-permute-start(f32[16,1280]{1,0:T(8,128)} %refs_0_.2), channel_id=1, source_target_pairs={{0,16},{16,0},{1,17},{17,1},{2,18},{18,2},{3,19},{19,3},{4,20},{20... | collective-permute-start | bytes 245768 | tf_op jit(solution)/shard_map/ppermute | solution.py:288
  6.4 13.0 %collective-permute-start.4 = (f32[16,1280]{1,0:T(8,128)S(1)}, f32[16,1280]{1,0:T(8,128)S(1)}, u32[]{:S(2)}, u32[]{:S(2)}) collective-permute-start(f32[16,1280]{1,0:T(8,128)S(1)} %collective-permute-done.refs_1_), channel_id=1, source_target_pairs={{0,16},{16,0},{1,17},{17,1},{2,18},{18,2},{3,19},{19,3},{4,20},{20... | collective-permute-start | bytes 245768 | tf_op jit(solution)/shard_map/ppermute | solution.py:288
  13.2 6.2 %collective-permute-start.5 = (f32[16,1280]{1,0:T(8,128)S(1)}, f32[16,1280]{1,0:T(8,128)S(1)}, u32[]{:S(2)}, u32[]{:S(2)}) collective-permute-start(f32[16,1280]{1,0:T(8,128)S(1)} %collective-permute-done.1.refs_2_), channel_id=1, source_target_pairs={{0,16},{16,0},{1,17},{17,1},{2,18},{18,2},{3,19},{19,3},{4,20},{20... | collective-permute-start | bytes 245768 | tf_op jit(solution)/shard_map/ppermute | solution.py:288
  13.2 6.2 %collective-permute-start.6 = (f32[16,1280]{1,0:T(8,128)S(1)}, f32[16,1280]{1,0:T(8,128)S(1)}, u32[]{:S(2)}, u32[]{:S(2)}) collective-permute-start(f32[16,1280]{1,0:T(8,128)S(1)} %collective-permute-done.2.refs_3_), channel_id=1, source_target_pairs={{0,16},{16,0},{1,17},{17,1},{2,18},{18,2},{3,19},{19,3},{4,20},{20... | collective-permute-start | bytes 245768 | tf_op jit(solution)/shard_map/ppermute | solution.py:288
  22.8 8.5 %collective-permute-start.7 = (f32[2,64,864]{2,1,0:T(8,128)S(1)}, f32[2,64,864]{2,1,0:T(8,128)S(1)}, u32[]{:S(2)}, u32[]{:S(2)}) collective-permute-start(f32[2,64,864]{2,1,0:T(8,128)S(1)} %get-tuple-element.47), channel_id=1, source_target_pairs={{0,4},{4,0},{8,12},{12,8},{16,24},{20,28},{24,16},{28,20},{1,5},{5... | collective-permute-start | bytes 1327112 | tf_op jit(solution)/shard_map/ppermute | solution.py:293
  24.4 8.6 %collective-permute-start.15 = (f32[16,1280]{1,0:T(8,128)S(1)}, f32[16,1280]{1,0:T(8,128)S(1)}, u32[]{:S(2)}, u32[]{:S(2)}) collective-permute-start(f32[16,1280]{1,0:T(8,128)S(1)} %copy-done.1), channel_id=1, source_target_pairs={{0,1},{1,0},{2,3},{3,2},{4,5},{5,4},{6,7},{7,6},{8,9},{9,8},{10,11... | collective-permute-start | bytes 245768 | tf_op jit(solution)/shard_map/ppermute | solution.py:285
  25.3 9.5 %collective-permute-start.16 = (f32[16,1280]{1,0:T(8,128)S(1)}, f32[16,1280]{1,0:T(8,128)S(1)}, u32[]{:S(2)}, u32[]{:S(2)}) collective-permute-start(f32[16,1280]{1,0:T(8,128)S(1)} %copy-done.1), channel_id=1, source_target_pairs={{0,2},{1,3},{2,0},{3,1},{4,6},{5,7},{6,4},{7,5},{8,10},{9,11},{10,... | collective-permute-start | bytes 245768 | tf_op jit(solution)/shard_map/ppermute | solution.py:285
  27.4 7.4 %collective-permute-start.17 = (f32[16,1280]{1,0:T(8,128)S(1)}, f32[16,1280]{1,0:T(8,128)S(1)}, u32[]{:S(2)}, u32[]{:S(2)}) collective-permute-start(f32[16,1280]{1,0:T(8,128)S(1)} %copy-done.1), channel_id=1, source_target_pairs={{0,3},{1,2},{2,1},{3,0},{4,7},{5,6},{6,5},{7,4},{8,11},{9,10},{10,... | collective-permute-start | bytes 245768 | tf_op jit(solution)/shard_map/ppermute | solution.py:285
  31.4 7.8 %collective-permute-start.8 = (f32[2,32,864]{2,1,0:T(8,128)S(1)}, f32[2,32,864]{2,1,0:T(8,128)S(1)}, u32[]{:S(2)}, u32[]{:S(2)}) collective-permute-start(f32[2,32,864]{2,1,0:T(8,128)S(1)} %get-tuple-element.49), channel_id=1, source_target_pairs={{0,8},{4,12},{8,0},{12,4},{16,20},{20,16},{24,28},{28,24},{1,9},{5... | collective-permute-start | bytes 663560 | tf_op jit(solution)/shard_map/ppermute | solution.py:293
  38.4 8.4 %collective-permute-start.22 = (f32[1,64,864]{2,1,0:T(8,128)S(1)}, f32[1,64,864]{2,1,0:T(8,128)S(1)}, u32[]{:S(2)}, u32[]{:S(2)}) collective-permute-start(f32[1,64,864]{2,1,0:T(8,128)S(1)} %get-tuple-element.59), channel_id=1, source_target_pairs={{0,4},{4,0},{8,12},{12,8},{16,24},{20,28},{24,16},{28,20},{1,5},{5... | collective-permute-start | bytes 663560 | tf_op jit(solution)/shard_map/ppermute | solution.py:293
  39.2 9.8 %collective-permute-start.9 = (f32[2,32,864]{2,1,0:T(8,128)S(1)}, f32[2,32,864]{2,1,0:T(8,128)S(1)}, u32[]{:S(2)}, u32[]{:S(2)}) collective-permute-start(f32[2,32,864]{2,1,0:T(8,128)S(1)} %shard_map.95.refs_0_), channel_id=1, source_target_pairs={{0,8},{4,12},{8,0},{12,4},{16,20},{20,16},{24,28},{28,24},{1,9},{5... | collective-permute-start | bytes 663560 | tf_op jit(solution)/shard_map/ppermute | solution.py:293
  46.8 6.1 %collective-permute-start.23 = (f32[1,32,864]{2,1,0:T(8,128)S(1)}, f32[1,32,864]{2,1,0:T(8,128)S(1)}, u32[]{:S(2)}, u32[]{:S(2)}) collective-permute-start(f32[1,32,864]{2,1,0:T(8,128)S(1)} %get-tuple-element.61), channel_id=1, source_target_pairs={{0,8},{4,12},{8,0},{12,4},{16,20},{20,16},{24,28},{28,24},{1,9},{5... | collective-permute-start | bytes 331784 | tf_op jit(solution)/shard_map/ppermute | solution.py:293
  47.0 12.4 %collective-permute-start.10 = (f32[2,32,864]{2,1,0:T(8,128)S(1)}, f32[2,32,864]{2,1,0:T(8,128)S(1)}, u32[]{:S(2)}, u32[]{:S(2)}) collective-permute-start(f32[2,32,864]{2,1,0:T(8,128)S(1)} %shard_map.95.refs_0_), channel_id=1, source_target_pairs={{0,4},{4,0},{8,12},{12,8},{16,24},{20,28},{24,16},{28,20},{1,5},{5... | collective-permute-start | bytes 663560 | tf_op jit(solution)/shard_map/ppermute | solution.py:293
  49.0 10.4 %collective-permute-start.11 = (f32[2,32,864]{2,1,0:T(8,128)S(1)}, f32[2,32,864]{2,1,0:T(8,128)S(1)}, u32[]{:S(2)}, u32[]{:S(2)}) collective-permute-start(f32[2,32,864]{2,1,0:T(8,128)S(1)} %collective-permute-done.9.refs_1_), channel_id=1, source_target_pairs={{0,4},{4,0},{8,12},{12,8},{16,24},{20,28},{24,16},{28,20},{1,5},{5... | collective-permute-start | bytes 663560 | tf_op jit(solution)/shard_map/ppermute | solution.py:293
  52.9 6.0 %collective-permute-start.24 = (f32[1,32,864]{2,1,0:T(8,128)S(1)}, f32[1,32,864]{2,1,0:T(8,128)S(1)}, u32[]{:S(2)}, u32[]{:S(2)}) collective-permute-start(f32[1,32,864]{2,1,0:T(8,128)S(1)} %shard_map.101.refs_0_), channel_id=1, source_target_pairs={{0,8},{4,12},{8,0},{12,4},{16,20},{20,16},{24,28},{28,24},{1,9},{5... | collective-permute-start | bytes 331784 | tf_op jit(solution)/shard_map/ppermute | solution.py:293
  53.1 8.2 %collective-permute-start.25 = (f32[1,32,864]{2,1,0:T(8,128)S(1)}, f32[1,32,864]{2,1,0:T(8,128)S(1)}, u32[]{:S(2)}, u32[]{:S(2)}) collective-permute-start(f32[1,32,864]{2,1,0:T(8,128)S(1)} %shard_map.101.refs_0_), channel_id=1, source_target_pairs={{0,4},{4,0},{8,12},{12,8},{16,24},{20,28},{24,16},{28,20},{1,5},{5... | collective-permute-start | bytes 331784 | tf_op jit(solution)/shard_map/ppermute | solution.py:293
  66.5 19.3 %collective-permute-start.31 = (f32[864,256]{1,0:T(8,128)S(1)}, f32[864,256]{1,0:T(8,128)S(1)}, u32[]{:S(2)}, u32[]{:S(2)}) collective-permute-start(f32[864,256]{1,0:T(8,128)S(1)} %get-tuple-element.72.own), channel_id=1, source_target_pairs={{0,16},{16,0},{1,17},{17,1},{2,18},{18,2},{3,19},{19,3},{4,20},{20... | collective-permute-start | bytes 2654216 | tf_op jit(solution)/shard_map/ppermute | solution.py:288
  69.5 6.8 %collective-permute-start.13 = (f32[1,32,1280]{2,1,0:T(8,128)S(1)}, f32[1,32,1280]{2,1,0:T(8,128)S(1)}, u32[]{:S(2)}, u32[]{:S(2)}) collective-permute-start(f32[1,32,1280]{2,1,0:T(8,128)S(1)} %get-tuple-element.55), channel_id=1, source_target_pairs={{0,1},{1,0},{2,3},{3,2},{4,5},{5,4},{6,7},{7,6},{8,9},{9,8},{10,11... | collective-permute-start | bytes 491528 | tf_op jit(solution)/shard_map/ppermute | solution.py:285
  70.6 9.3 %collective-permute-start.28 = (f32[16,1280]{1,0:T(8,128)S(1)}, f32[16,1280]{1,0:T(8,128)S(1)}, u32[]{:S(2)}, u32[]{:S(2)}) collective-permute-start(f32[16,1280]{1,0:T(8,128)S(1)} %bitcast.30), channel_id=1, source_target_pairs={{0,3},{1,2},{2,1},{3,0},{4,7},{5,6},{6,5},{7,4},{8,11},{9,10},{10,... | collective-permute-start | bytes 245768 | tf_op jit(solution)/shard_map/ppermute | solution.py:285
  73.2 9.7 %collective-permute-start.29 = (f32[16,1280]{1,0:T(8,128)S(1)}, f32[16,1280]{1,0:T(8,128)S(1)}, u32[]{:S(2)}, u32[]{:S(2)}) collective-permute-start(f32[16,1280]{1,0:T(8,128)S(1)} %bitcast.29), channel_id=1, source_target_pairs={{0,2},{1,3},{2,0},{3,1},{4,6},{5,7},{6,4},{7,5},{8,10},{9,11},{10,... | collective-permute-start | bytes 245768 | tf_op jit(solution)/shard_map/ppermute | solution.py:285
  73.2 9.7 %collective-permute-start.30 = (f32[16,1280]{1,0:T(8,128)S(1)}, f32[16,1280]{1,0:T(8,128)S(1)}, u32[]{:S(2)}, u32[]{:S(2)}) collective-permute-start(f32[16,1280]{1,0:T(8,128)S(1)} %bitcast.28), channel_id=1, source_target_pairs={{0,1},{1,0},{2,3},{3,2},{4,5},{5,4},{6,7},{7,6},{8,9},{9,8},{10,11... | collective-permute-start | bytes 245768 | tf_op jit(solution)/shard_map/ppermute | solution.py:285
  76.3 8.8 %collective-permute-start.14 = (f32[1,16,1280]{2,1,0:T(8,128)S(1)}, f32[1,16,1280]{2,1,0:T(8,128)S(1)}, u32[]{:S(2)}, u32[]{:S(2)}) collective-permute-start(f32[1,16,1280]{2,1,0:T(8,128)S(1)} %get-tuple-element.57), channel_id=1, source_target_pairs={{0,2},{1,3},{2,0},{3,1},{4,6},{5,7},{6,4},{7,5},{8,10},{9,11},{10,... | collective-permute-start | bytes 245768 | tf_op jit(solution)/shard_map/ppermute | solution.py:285
  (10 other events, 35.0 us)

commit v2 on v1

--- a/solution.py
+++ b/solution.py
@@ -37,6 +37,13 @@
     rows = both.shape[0] // 2
     wide = mm(both, w_high, dims)
     return wide[:rows] + wide[rows:] + mm(both[:rows], w_low, dims)
+
+
+def turned_product(both, w_high, w_low):
+    rows = both.shape[0] // 2
+    dims = ((1,), (1,))
+    wide = mm(w_high, both, dims)
+    return (wide[:, :rows] + wide[:, rows:] + mm(w_low, both[:rows], dims)).T
 
 
 def tiles(extent):
@@ -112,7 +119,7 @@
     stack[...] = both if half == both.shape[1] else jnp.where(replica == 0, both[:, :half], both[:, half:])
     outs = list(zip((send, keep), with_bit(list(range(n)), 1)))
     for i in range(count):
-        part_ref[...] = product(both, weights[2 * i][...], weights[2 * i + 1][...], ((1,), (1,)))
+        part_ref[...] = turned_product(both, weights[2 * i][...], weights[2 * i + 1][...])
         for ref, chosen in outs:
             for place, label in enumerate(chosen):
                 for k in range(2):
@@ -196,26 +203,36 @@
     return [(at, end - at) for at, end in zip(cuts, cuts[1:])]
 
 
-def weights_kernel(scal, own, far, x_right, h_left, y_right, g_out, u_out, d_out, g_buffer, u_buffer, d_buffer, sems):
-    lines, rows = own.shape[0], own.shape[1] // 2
+def writer(sems):
     copies = []
 
     def send(buffer, out, start, size):
-        rows_at = pl.ds(pl.multiple_of(start, 8), size)
-        copy = pltpu.make_async_copy(buffer, out.at[rows_at, :], sems.at[len(copies)])
+        rows = pl.ds(pl.multiple_of(start, 8), size)
+        copy = pltpu.make_async_copy(buffer, out.at[rows, :], sems.at[len(copies)])
         copy.start()
         copies.append(copy)
 
-    for at, size in pieces(lines):
-        piece = d_buffer.at[pl.ds(at, size), :]
-        d_buffer[at : at + size, :] = outer(h_left[at : at + size, :], y_right[...])
-        send(piece, d_out, at, size)
+    return copies, send
+
+
+def down_kernel(left, right, out, buffer, sems):
+    copies, send = writer(sems)
+    for at, size in pieces(left.shape[0]):
+        buffer[at : at + size, :] = outer(left[at : at + size, :], right[...])
+        send(buffer.at[pl.ds(at, size), :], out, at, size)
+    for copy in copies:
+        copy.wait()
+
+
+def weights_kernel(scal, own, far, right, g_out, u_out, g_buffer, u_buffer, sems):
+    lines, rows = own.shape[0], own.shape[1] // 2
+    copies, send = writer(sems)
     for out, buffer, first in ((g_out, g_buffer, 0), (u_out, u_buffer, rows)):
         for k, (source, which) in enumerate(((own, scal[0]), (far, 1 - scal[0]))):
             for at, size in pieces(lines):
                 left = jnp.concatenate(split(source[at : at + size, first : first + rows]), axis=1)
                 here = k * lines + at
-                buffer[here : here + size, :] = outer(left, x_right[...])
+                buffer[here : here + size, :] = outer(left, right[...])
                 send(buffer.at[pl.ds(here, size), :], out, which * lines + at, size)
     for copy in copies:
         copy.wait()
@@ -306,7 +323,10 @@
                 send, keep = add_groups(keep, got, group, picks)
         held = [([0], add_groups(keep, got, group, [[0]])[0])]
         for level in reversed(range(levels)):
-            held = held + [([p ^ (1 << level) for p in some], hop(value, level)) for some, value in held]
+            held = held + [
+                ([p ^ (1 << level) for p in some], hop(value, level))
+                for some, value in held
+            ]
         return [value for _, value in held], [some for some, _ in held]
 
     def to_owner(keep, send):
@@ -361,16 +381,27 @@
     far = swap(grads)
     token_parts = to_owner(keep, send)
 
-    shapes = [(full, half_width), (full, half_width), (hidden, depth)]
-    grad_gate, grad_up, grad_down = call(
+    (grad_down,) = call(
+        down_kernel,
+        [shape_of((hidden, depth))],
+        [hid_turned, y_both],
+        [VMEM] * 2,
+        [pltpu.VMEM((hidden, depth), F32), pltpu.SemaphoreType.DMA((4,))],
+        6 * rows * hidden * depth,
+        4 * hidden * depth,
+        10,
+        HBM,
+    )
+    shapes = [(full, half_width)] * 2
+    grad_gate, grad_up = call(
         weights_kernel,
         [shape_of(shape) for shape in shapes],
-        [scal, grads, far, x_half, hid_turned, y_both],
-        [SMEM] + [VMEM] * 5,
-        [pltpu.VMEM(shape, F32) for shape in shapes] + [pltpu.SemaphoreType.DMA((20,))],
-        18 * rows * half_width * full,
-        12 * half_width * full,
-        20,
+        [scal, grads, far, x_half],
+        [SMEM] + [VMEM] * 3,
+        [pltpu.VMEM(shape, F32) for shape in shapes] + [pltpu.SemaphoreType.DMA((16,))],
+        12 * rows * half_width * full,
+        8 * half_width * full,
+        16,
         HBM,
     )
     output, grad_tokens = finish([output_parts, token_parts])

time: 92 us -> 90.2 us (0.980)
  waiting for transfers between devices: 37.2 us -> 34.6 us
    ppermute x11, waiting for transfers between devices: 15.2 us -> 12.5 us  [shift(): return lax.ppermute(value, 'hid', [(i, i ^ s) for i in range(n)])]
    pallas_call x14 -> x15, Pallas kernels: 22.6 us -> 23.5 us  [call(): pl.pallas_call(body, out_shape=out_shape, in_specs=in_specs, out_specs=[o...]
  transfers between devices with their start and end apart: 32 -> 32, of which waited for: 15 -> 14; matrix products, arithmetic and copies ran while one was open for 0% -> 0% of each run, Pallas kernels for 11% -> 15%
where the time goes in v2:
time: 90.2 us; the launch traced here: 90.1 us
  waiting for transfers between devices  34.6 us (38%)
  starting transfers between devices  30.9 us (34%)
  Pallas kernels  23.5 us (26%)
  between operations  0.96 us (1%)
    pallas_call x15, Pallas kernels, call(): pl.pallas_call(body, out_shape=out_shape, in_specs=in_specs, out_specs=[o...  23.5 us
    ppermute x10, waiting for transfers between devices, hop(): return lax.ppermute(value, ('rep', 'width'), pairs)  18.8 us
    ppermute x11, starting transfers between devices, shift(): return lax.ppermute(value, 'hid', [(i, i ^ s) for i in range(n)])  18 us
    ppermute x11, waiting for transfers between devices, shift(): return lax.ppermute(value, 'hid', [(i, i ^ s) for i in range(n)])  12.5 us
    ppermute x10, starting transfers between devices, hop(): return lax.ppermute(value, ('rep', 'width'), pairs)  10.3 us
    ppermute x11, waiting for transfers between devices, swap(): return lax.ppermute(value, 'rep', [(0, 1), (1, 0)])  3.24 us
    ppermute x11, starting transfers between devices, swap(): return lax.ppermute(value, 'rep', [(0, 1), (1, 0)])  2.63 us
  transfers between devices with their start and end apart: 32, of which 14 were waited for; matrix products, arithmetic and copies ran while one was open for 0% of the time, Pallas kernels for 15%

profile of v2, /device:TPU:0, one launch (start us, length us, event | category | flops | bytes accessed | tf_op | source)
XLA Modules:
  0.0 90.1 jit_solution(3372096457085006939)
XLA Ops:
  0.6 3.1 %collective-permute-start = (f32[16,1280]{1,0:T(8,128)}, f32[16,1280]{1,0:T(8,128)S(1)}, u32[]{:S(2)}, u32[]{:S(2)}) collective-permute-start(f32[16,1280]{1,0:T(8,128)} %refs_0_.2), channel_id=1, source_target_pairs={{0,1},{1,0},{2,3},{3,2},{4,5},{5,4},{6,7},{7,6},{8,9},{9,8},{10,11... | collective-permute-start | bytes 245768 | tf_op jit(solution)/shard_map/ppermute | solution.py:302
  3.7 2.6 %collective-permute-start.1 = (f32[16,1280]{1,0:T(8,128)}, f32[16,1280]{1,0:T(8,128)S(1)}, u32[]{:S(2)}, u32[]{:S(2)}) collective-permute-start(f32[16,1280]{1,0:T(8,128)} %refs_0_.2), channel_id=1, source_target_pairs={{0,2},{1,3},{2,0},{3,1},{4,6},{5,7},{6,4},{7,5},{8,10},{9,11},{10,... | collective-permute-start | bytes 245768 | tf_op jit(solution)/shard_map/ppermute | solution.py:302
  6.9 6.3 %collective-permute-done.1.refs_2_ = f32[16,1280]{1,0:T(8,128)S(1)} collective-permute-done((f32[16,1280]{1,0:T(8,128)}, f32[16,1280]{1,0:T(8,128)S(1)}, u32[]{:S(2)}, u32[]{:S(2)}) %collective-permute-start.1) | collective-permute-done | bytes 81952 | tf_op jit(solution)/shard_map/ppermute | solution.py:302
  13.8 5.6 %shard_map.92 = (bf16[864,1280]{1,0:T(8,128)(2,1)S(1)}, bf16[864,1280]{1,0:T(8,128)(2,1)S(1)}, bf16[864,1280]{1,0:T(8,128)(2,1)S(1)}, bf16[864,1280]{1,0:T(8,128...) custom-call(s32[2]{0:T(128)S(1)} %pad_add_fusion.scal, f32[1728,1280]{1,0:T(8,128)} %bitcast.31, ...), custom_call_target="tpu_custom_call" | custom-call | flops 19906560 | bytes 26542080 | tf_op jit(solution)/shard_map/pallas_call | solution.py:54
  19.4 3.2 %shard_map.93 = (f32[2,64,864]{2,1,0:T(8,128)S(1)}, f32[2,64,864]{2,1,0:T(8,128)S(1)}, bf16[256,640]{1,0:T(8,128)(2,1)S(1)}) custom-call(s32[2]{0:T(128)S(1)} %pad_add_fusion.scal, f32[16,1280]{1,0:T(8,128)S(1)} %copy-done, f32[16,1280]{1,0:T(8,128)S(1)} %collective-permute-done.refs_1_, f32[16,1280]{1,0:T(8,128)S(1)} %collective-permute-done.1.refs_2_, ...), custom_call_target="tpu_custom_call" | custom-call | flops 1698693120 | bytes 8847360 | tf_op jit(solution)/shard_map/pallas_call | solution.py:54
  25.1 2.1 %collective-permute-start.16 = (f32[16,1280]{1,0:T(8,128)S(1)}, f32[16,1280]{1,0:T(8,128)S(1)}, u32[]{:S(2)}, u32[]{:S(2)}) collective-permute-start(f32[16,1280]{1,0:T(8,128)S(1)} %copy-done.1), channel_id=1, source_target_pairs={{0,2},{1,3},{2,0},{3,1},{4,6},{5,7},{6,4},{7,5},{8,10},{9,11},{10,... | collective-permute-start | bytes 245768 | tf_op jit(solution)/shard_map/ppermute | solution.py:302
  28.6 2.6 %collective-permute-done.7.got = f32[2,64,864]{2,1,0:T(8,128)S(1)} collective-permute-done((f32[2,64,864]{2,1,0:T(8,128)S(1)}, f32[2,64,864]{2,1,0:T(8,128)S(1)}, u32[]{:S(2)}, u32[]{:S(2)}) %collective-permute-start.7) | collective-permute-done | bytes 442400 | tf_op jit(solution)/shard_map/ppermute | solution.py:310
  31.2 1.6 %collective-permute-start.8 = (f32[2,32,864]{2,1,0:T(8,128)S(1)}, f32[2,32,864]{2,1,0:T(8,128)S(1)}, u32[]{:S(2)}, u32[]{:S(2)}) collective-permute-start(f32[2,32,864]{2,1,0:T(8,128)S(1)} %get-tuple-element.48), channel_id=1, source_target_pairs={{0,8},{4,12},{8,0},{12,4},{16,20},{20,16},{24,28},{28,24},{1,9},{5... | collective-permute-start | bytes 663560 | tf_op jit(solution)/shard_map/ppermute | solution.py:310
  36.1 2.0 %shard_map.99 = (f32[1,64,864]{2,1,0:T(8,128)S(1)}, f32[1,64,864]{2,1,0:T(8,128)S(1)}, bf16[256,1280]{1,0:T(8,128)(2,1)S(1)}) custom-call(s32[2]{0:T(128)S(1)} %pad_add_fusion.scal, f32[16,1280]{1,0:T(8,128)S(1)} %copy-done.1, f32[16,1280]{1,0:T(8,128)S(1)} %collective-permute-done.15.refs_1_, f32[16,1280]{1,0:T(8,128)S(1)} %collective-permute-done.16.refs_2_, ...), custom_call_target="tpu_custom_call" | custom-call | flops 849346560 | bytes 4423680 | tf_op jit(solution)/shard_map/pallas_call | solution.py:54
  40.3 6.2 %collective-permute-done.22.got = f32[1,64,864]{2,1,0:T(8,128)S(1)} collective-permute-done((f32[1,64,864]{2,1,0:T(8,128)S(1)}, f32[1,64,864]{2,1,0:T(8,128)S(1)}, u32[]{:S(2)}, u32[]{:S(2)}) %collective-permute-start.22) | collective-permute-done | bytes 221216 | tf_op jit(solution)/shard_map/ppermute | solution.py:310
  46.7 2.0 %collective-permute-start.10 = (f32[2,32,864]{2,1,0:T(8,128)S(1)}, f32[2,32,864]{2,1,0:T(8,128)S(1)}, u32[]{:S(2)}, u32[]{:S(2)}) collective-permute-start(f32[2,32,864]{2,1,0:T(8,128)S(1)} %shard_map.95.refs_0_), channel_id=1, source_target_pairs={{0,4},{4,0},{8,12},{12,8},{16,24},{20,28},{24,16},{28,20},{1,5},{5... | collective-permute-start | bytes 663560 | tf_op jit(solution)/shard_map/ppermute | solution.py:310
  48.8 3.8 %collective-permute-done.23.got = f32[1,32,864]{2,1,0:T(8,128)S(1)} collective-permute-done((f32[1,32,864]{2,1,0:T(8,128)S(1)}, f32[1,32,864]{2,1,0:T(8,128)S(1)}, u32[]{:S(2)}, u32[]{:S(2)}) %collective-permute-start.23) | collective-permute-done | bytes 110624 | tf_op jit(solution)/shard_map/ppermute | solution.py:310
  52.9 2.0 %collective-permute-start.25 = (f32[1,32,864]{2,1,0:T(8,128)S(1)}, f32[1,32,864]{2,1,0:T(8,128)S(1)}, u32[]{:S(2)}, u32[]{:S(2)}) collective-permute-start(f32[1,32,864]{2,1,0:T(8,128)S(1)} %shard_map.101.refs_0_), channel_id=1, source_target_pairs={{0,4},{4,0},{8,12},{12,8},{16,24},{20,28},{24,16},{28,20},{1,5},{5... | collective-permute-start | bytes 331784 | tf_op jit(solution)/shard_map/ppermute | solution.py:310
  54.9 3.8 %collective-permute-done.24.refs_1_ = f32[1,32,864]{2,1,0:T(8,128)S(1)} collective-permute-done((f32[1,32,864]{2,1,0:T(8,128)S(1)}, f32[1,32,864]{2,1,0:T(8,128)S(1)}, u32[]{:S(2)}, u32[]{:S(2)}) %collective-permute-start.24) | collective-permute-done | bytes 110624 | tf_op jit(solution)/shard_map/ppermute | solution.py:310
  59.2 1.9 %shard_map.96 = (f32[64,1280]{1,0:T(8,128)S(1)}, f32[64,1280]{1,0:T(8,128)S(1)}, bf16[864,256]{1,0:T(8,128)(2,1)S(1)}, f32[128,864]{1,0:T(8,128)S(1)}, f32[128,864]{1,0:T(8,128)S(1)}) custom-call(s32[2]{0:T(128)S(1)} %pad_add_fusion.scal, f32[2,32,864]{2,1,0:T(8,128)S(1)} %shard_map.95.refs_0_, f32[2,32,864]{2,1,0:T(8,128)S(1)} %collective-permute-done.9.refs_1_, ...), custom_call_target="tpu_custom_call" | custom-call | flops 849346560 | bytes 4423680 | tf_op jit(solution)/shard_map/pallas_call | solution.py:54
  61.0 2.4 %collective-permute-done.26.refs_3_ = f32[1,32,864]{2,1,0:T(8,128)S(1)} collective-permute-done((f32[1,32,864]{2,1,0:T(8,128)S(1)}, f32[1,32,864]{2,1,0:T(8,128)S(1)}, u32[]{:S(2)}, u32[]{:S(2)}) %collective-permute-start.26) | collective-permute-done | bytes 110624 | tf_op jit(solution)/shard_map/ppermute | solution.py:310
  63.5 2.8 %shard_map.102 = (f32[64,1280]{1,0:T(8,128)S(1)}, f32[64,1280]{1,0:T(8,128)S(1)}, f32[864,256]{1,0:T(8,128)S(1)}) custom-call(s32[2]{0:T(128)S(1)} %pad_add_fusion.scal, f32[1,32,864]{2,1,0:T(8,128)S(1)} %shard_map.101.refs_0_, f32[1,32,864]{2,1,0:T(8,128)S(1)} %collective-permute-done.24.refs_1_, f32[1,32,864]{2,1,0:T(8,128)S(1)} %collective-permute-done.25.refs_2_, ...), custom_call_target="tpu_custom_call" | custom-call | flops 1698693120 | bytes 8847360 | tf_op jit(solution)/shard_map/pallas_call | solution.py:54
  66.9 2.3 %collective-permute-done.12 = f32[64,1280]{1,0:T(8,128)S(1)} collective-permute-done((f32[64,1280]{1,0:T(8,128)S(1)}, f32[64,1280]{1,0:T(8,128)S(1)}, u32[]{:S(2)}, u32[]{:S(2)}) %collective-permute-start.12) | collective-permute-done | bytes 327712 | tf_op jit(solution)/shard_map/ppermute | solution.py:305
  70.3 2.5 %collective-permute-start.28 = (f32[16,1280]{1,0:T(8,128)S(1)}, f32[16,1280]{1,0:T(8,128)S(1)}, u32[]{:S(2)}, u32[]{:S(2)}) collective-permute-start(f32[16,1280]{1,0:T(8,128)S(1)} %bitcast.30), channel_id=1, source_target_pairs={{0,3},{1,2},{2,1},{3,0},{4,7},{5,6},{6,5},{7,4},{8,11},{9,10},{10,... | collective-permute-start | bytes 245768 | tf_op jit(solution)/shard_map/ppermute | solution.py:302
  72.9 1.9 %collective-permute-start.30 = (f32[16,1280]{1,0:T(8,128)S(1)}, f32[16,1280]{1,0:T(8,128)S(1)}, u32[]{:S(2)}, u32[]{:S(2)}) collective-permute-start(f32[16,1280]{1,0:T(8,128)S(1)} %bitcast.28), channel_id=1, source_target_pairs={{0,1},{1,0},{2,3},{3,2},{4,5},{5,4},{6,7},{7,6},{8,9},{9,8},{10,11... | collective-permute-start | bytes 245768 | tf_op jit(solution)/shard_map/ppermute | solution.py:302
  76.1 2.4 %collective-permute-start.14 = (f32[1,16,1280]{2,1,0:T(8,128)S(1)}, f32[1,16,1280]{2,1,0:T(8,128)S(1)}, u32[]{:S(2)}, u32[]{:S(2)}) collective-permute-start(f32[1,16,1280]{2,1,0:T(8,128)S(1)} %get-tuple-element.56), channel_id=1, source_target_pairs={{0,2},{1,3},{2,0},{3,1},{4,6},{5,7},{6,4},{7,5},{8,10},{9,11},{10,... | collective-permute-start | bytes 245768 | tf_op jit(solution)/shard_map/ppermute | solution.py:302
  78.5 2.7 %shard_map.106 = f32[864,1280]{1,0:T(8,128)} custom-call(bf16[864,256]{1,0:T(8,128)(2,1)S(1)} %get-tuple-element.75.left, bf16[256,1280]{1,0:T(8,128)(2,1)S(1)} %get-tuple-element.76.right), custom_call_target="tpu_custom_call" | custom-call | flops 849346560 | bytes 4423680 | tf_op jit(solution)/shard_map/pallas_call | solution.py:54
  82.6 2.2 %collective-permute-done.14 = f32[1,16,1280]{2,1,0:T(8,128)S(1)} collective-permute-done((f32[1,16,1280]{2,1,0:T(8,128)S(1)}, f32[1,16,1280]{2,1,0:T(8,128)S(1)}, u32[]{:S(2)}, u32[]{:S(2)}) %collective-permute-start.14) | collective-permute-done | bytes 81952 | tf_op jit(solution)/shard_map/ppermute | solution.py:302
  85.5 4.4 %shard_map.105 = (f32[1728,640]{1,0:T(8,128)}, f32[1728,640]{1,0:T(8,128)}) custom-call(s32[2]{0:T(128)S(1)} %pad_add_fusion.scal, f32[864,256]{1,0:T(8,128)S(1)} %get-tuple-element.71.own, f32[864,256]{1,0:T(8,128)S(1)} %collective-permute-done.31.far, bf16[256,640]{1,0:T(8,128)(2,1)S(1)} %get-tuple-element.72.right), custom_call_target="tpu_custom_call" | custom-call | flops 1698693120 | bytes 8847360 | tf_op jit(solution)/shard_map/pallas_call | solution.py:54
  (60 shorter events, 16.6 us)
Async XLA Ops:
  3.7 9.4 %collective-permute-start.1 = (f32[16,1280]{1,0:T(8,128)}, f32[16,1280]{1,0:T(8,128)S(1)}, u32[]{:S(2)}, u32[]{:S(2)}) collective-permute-start(f32[16,1280]{1,0:T(8,128)} %refs_0_.2), channel_id=1, source_target_pairs={{0,2},{1,3},{2,0},{3,1},{4,6},{5,7},{6,4},{7,5},{8,10},{9,11},{10,... | collective-permute-start | bytes 245768 | tf_op jit(solution)/shard_map/ppermute | solution.py:302
  6.3 6.8 %collective-permute-start.2 = (f32[16,1280]{1,0:T(8,128)}, f32[16,1280]{1,0:T(8,128)S(1)}, u32[]{:S(2)}, u32[]{:S(2)}) collective-permute-start(f32[16,1280]{1,0:T(8,128)} %refs_0_.2), channel_id=1, source_target_pairs={{0,3},{1,2},{2,1},{3,0},{4,7},{5,6},{6,5},{7,4},{8,11},{9,10},{10,... | collective-permute-start | bytes 245768 | tf_op jit(solution)/shard_map/ppermute | solution.py:302
  6.3 13.0 %collective-permute-start.3 = (f32[16,1280]{1,0:T(8,128)}, f32[16,1280]{1,0:T(8,128)S(1)}, u32[]{:S(2)}, u32[]{:S(2)}) collective-permute-start(f32[16,1280]{1,0:T(8,128)} %refs_0_.2), channel_id=1, source_target_pairs={{0,16},{16,0},{1,17},{17,1},{2,18},{18,2},{3,19},{19,3},{4,20},{20... | collective-permute-start | bytes 245768 | tf_op jit(solution)/shard_map/ppermute | solution.py:305
  6.4 13.0 %collective-permute-start.4 = (f32[16,1280]{1,0:T(8,128)S(1)}, f32[16,1280]{1,0:T(8,128)S(1)}, u32[]{:S(2)}, u32[]{:S(2)}) collective-permute-start(f32[16,1280]{1,0:T(8,128)S(1)} %collective-permute-done.refs_1_), channel_id=1, source_target_pairs={{0,16},{16,0},{1,17},{17,1},{2,18},{18,2},{3,19},{19,3},{4,20},{20... | collective-permute-start | bytes 245768 | tf_op jit(solution)/shard_map/ppermute | solution.py:305
  13.2 6.2 %collective-permute-start.5 = (f32[16,1280]{1,0:T(8,128)S(1)}, f32[16,1280]{1,0:T(8,128)S(1)}, u32[]{:S(2)}, u32[]{:S(2)}) collective-permute-start(f32[16,1280]{1,0:T(8,128)S(1)} %collective-permute-done.1.refs_2_), channel_id=1, source_target_pairs={{0,16},{16,0},{1,17},{17,1},{2,18},{18,2},{3,19},{19,3},{4,20},{20... | collective-permute-start | bytes 245768 | tf_op jit(solution)/shard_map/ppermute | solution.py:305
  13.2 6.2 %collective-permute-start.6 = (f32[16,1280]{1,0:T(8,128)S(1)}, f32[16,1280]{1,0:T(8,128)S(1)}, u32[]{:S(2)}, u32[]{:S(2)}) collective-permute-start(f32[16,1280]{1,0:T(8,128)S(1)} %collective-permute-done.2.refs_3_), channel_id=1, source_target_pairs={{0,16},{16,0},{1,17},{17,1},{2,18},{18,2},{3,19},{19,3},{4,20},{20... | collective-permute-start | bytes 245768 | tf_op jit(solution)/shard_map/ppermute | solution.py:305
  22.6 8.5 %collective-permute-start.7 = (f32[2,64,864]{2,1,0:T(8,128)S(1)}, f32[2,64,864]{2,1,0:T(8,128)S(1)}, u32[]{:S(2)}, u32[]{:S(2)}) collective-permute-start(f32[2,64,864]{2,1,0:T(8,128)S(1)} %get-tuple-element.46), channel_id=1, source_target_pairs={{0,4},{4,0},{8,12},{12,8},{16,24},{20,28},{24,16},{28,20},{1,5},{5... | collective-permute-start | bytes 1327112 | tf_op jit(solution)/shard_map/ppermute | solution.py:310
  24.2 8.6 %collective-permute-start.15 = (f32[16,1280]{1,0:T(8,128)S(1)}, f32[16,1280]{1,0:T(8,128)S(1)}, u32[]{:S(2)}, u32[]{:S(2)}) collective-permute-start(f32[16,1280]{1,0:T(8,128)S(1)} %copy-done.1), channel_id=1, source_target_pairs={{0,1},{1,0},{2,3},{3,2},{4,5},{5,4},{6,7},{7,6},{8,9},{9,8},{10,11... | collective-permute-start | bytes 245768 | tf_op jit(solution)/shard_map/ppermute | solution.py:302
  25.1 9.5 %collective-permute-start.16 = (f32[16,1280]{1,0:T(8,128)S(1)}, f32[16,1280]{1,0:T(8,128)S(1)}, u32[]{:S(2)}, u32[]{:S(2)}) collective-permute-start(f32[16,1280]{1,0:T(8,128)S(1)} %copy-done.1), channel_id=1, source_target_pairs={{0,2},{1,3},{2,0},{3,1},{4,6},{5,7},{6,4},{7,5},{8,10},{9,11},{10,... | collective-permute-start | bytes 245768 | tf_op jit(solution)/shard_map/ppermute | solution.py:302
  27.2 7.4 %collective-permute-start.17 = (f32[16,1280]{1,0:T(8,128)S(1)}, f32[16,1280]{1,0:T(8,128)S(1)}, u32[]{:S(2)}, u32[]{:S(2)}) collective-permute-start(f32[16,1280]{1,0:T(8,128)S(1)} %copy-done.1), channel_id=1, source_target_pairs={{0,3},{1,2},{2,1},{3,0},{4,7},{5,6},{6,5},{7,4},{8,11},{9,10},{10,... | collective-permute-start | bytes 245768 | tf_op jit(solution)/shard_map/ppermute | solution.py:302
  31.2 7.7 %collective-permute-start.8 = (f32[2,32,864]{2,1,0:T(8,128)S(1)}, f32[2,32,864]{2,1,0:T(8,128)S(1)}, u32[]{:S(2)}, u32[]{:S(2)}) collective-permute-start(f32[2,32,864]{2,1,0:T(8,128)S(1)} %get-tuple-element.48), channel_id=1, source_target_pairs={{0,8},{4,12},{8,0},{12,4},{16,20},{20,16},{24,28},{28,24},{1,9},{5... | collective-permute-start | bytes 663560 | tf_op jit(solution)/shard_map/ppermute | solution.py:310
  38.1 8.4 %collective-permute-start.22 = (f32[1,64,864]{2,1,0:T(8,128)S(1)}, f32[1,64,864]{2,1,0:T(8,128)S(1)}, u32[]{:S(2)}, u32[]{:S(2)}) collective-permute-start(f32[1,64,864]{2,1,0:T(8,128)S(1)} %get-tuple-element.58), channel_id=1, source_target_pairs={{0,4},{4,0},{8,12},{12,8},{16,24},{20,28},{24,16},{28,20},{1,5},{5... | collective-permute-start | bytes 663560 | tf_op jit(solution)/shard_map/ppermute | solution.py:310
  39.0 9.8 %collective-permute-start.9 = (f32[2,32,864]{2,1,0:T(8,128)S(1)}, f32[2,32,864]{2,1,0:T(8,128)S(1)}, u32[]{:S(2)}, u32[]{:S(2)}) collective-permute-start(f32[2,32,864]{2,1,0:T(8,128)S(1)} %shard_map.95.refs_0_), channel_id=1, source_target_pairs={{0,8},{4,12},{8,0},{12,4},{16,20},{20,16},{24,28},{28,24},{1,9},{5... | collective-permute-start | bytes 663560 | tf_op jit(solution)/shard_map/ppermute | solution.py:310
  46.5 6.1 %collective-permute-start.23 = (f32[1,32,864]{2,1,0:T(8,128)S(1)}, f32[1,32,864]{2,1,0:T(8,128)S(1)}, u32[]{:S(2)}, u32[]{:S(2)}) collective-permute-start(f32[1,32,864]{2,1,0:T(8,128)S(1)} %get-tuple-element.60), channel_id=1, source_target_pairs={{0,8},{4,12},{8,0},{12,4},{16,20},{20,16},{24,28},{28,24},{1,9},{5... | collective-permute-start | bytes 331784 | tf_op jit(solution)/shard_map/ppermute | solution.py:310
  46.7 12.4 %collective-permute-start.10 = (f32[2,32,864]{2,1,0:T(8,128)S(1)}, f32[2,32,864]{2,1,0:T(8,128)S(1)}, u32[]{:S(2)}, u32[]{:S(2)}) collective-permute-start(f32[2,32,864]{2,1,0:T(8,128)S(1)} %shard_map.95.refs_0_), channel_id=1, source_target_pairs={{0,4},{4,0},{8,12},{12,8},{16,24},{20,28},{24,16},{28,20},{1,5},{5... | collective-permute-start | bytes 663560 | tf_op jit(solution)/shard_map/ppermute | solution.py:310
  48.8 10.4 %collective-permute-start.11 = (f32[2,32,864]{2,1,0:T(8,128)S(1)}, f32[2,32,864]{2,1,0:T(8,128)S(1)}, u32[]{:S(2)}, u32[]{:S(2)}) collective-permute-start(f32[2,32,864]{2,1,0:T(8,128)S(1)} %collective-permute-done.9.refs_1_), channel_id=1, source_target_pairs={{0,4},{4,0},{8,12},{12,8},{16,24},{20,28},{24,16},{28,20},{1,5},{5... | collective-permute-start | bytes 663560 | tf_op jit(solution)/shard_map/ppermute | solution.py:310
  52.6 6.1 %collective-permute-start.24 = (f32[1,32,864]{2,1,0:T(8,128)S(1)}, f32[1,32,864]{2,1,0:T(8,128)S(1)}, u32[]{:S(2)}, u32[]{:S(2)}) collective-permute-start(f32[1,32,864]{2,1,0:T(8,128)S(1)} %shard_map.101.refs_0_), channel_id=1, source_target_pairs={{0,8},{4,12},{8,0},{12,4},{16,20},{20,16},{24,28},{28,24},{1,9},{5... | collective-permute-start | bytes 331784 | tf_op jit(solution)/shard_map/ppermute | solution.py:310
  52.9 8.2 %collective-permute-start.25 = (f32[1,32,864]{2,1,0:T(8,128)S(1)}, f32[1,32,864]{2,1,0:T(8,128)S(1)}, u32[]{:S(2)}, u32[]{:S(2)}) collective-permute-start(f32[1,32,864]{2,1,0:T(8,128)S(1)} %shard_map.101.refs_0_), channel_id=1, source_target_pairs={{0,4},{4,0},{8,12},{12,8},{16,24},{20,28},{24,16},{28,20},{1,5},{5... | collective-permute-start | bytes 331784 | tf_op jit(solution)/shard_map/ppermute | solution.py:310
  66.2 19.2 %collective-permute-start.31 = (f32[864,256]{1,0:T(8,128)S(1)}, f32[864,256]{1,0:T(8,128)S(1)}, u32[]{:S(2)}, u32[]{:S(2)}) collective-permute-start(f32[864,256]{1,0:T(8,128)S(1)} %get-tuple-element.71.own), channel_id=1, source_target_pairs={{0,16},{16,0},{1,17},{17,1},{2,18},{18,2},{3,19},{19,3},{4,20},{20... | collective-permute-start | bytes 2654216 | tf_op jit(solution)/shard_map/ppermute | solution.py:305
  69.2 6.8 %collective-permute-start.13 = (f32[1,32,1280]{2,1,0:T(8,128)S(1)}, f32[1,32,1280]{2,1,0:T(8,128)S(1)}, u32[]{:S(2)}, u32[]{:S(2)}) collective-permute-start(f32[1,32,1280]{2,1,0:T(8,128)S(1)} %get-tuple-element.54), channel_id=1, source_target_pairs={{0,1},{1,0},{2,3},{3,2},{4,5},{5,4},{6,7},{7,6},{8,9},{9,8},{10,11... | collective-permute-start | bytes 491528 | tf_op jit(solution)/shard_map/ppermute | solution.py:302
  70.3 10.9 %collective-permute-start.28 = (f32[16,1280]{1,0:T(8,128)S(1)}, f32[16,1280]{1,0:T(8,128)S(1)}, u32[]{:S(2)}, u32[]{:S(2)}) collective-permute-start(f32[16,1280]{1,0:T(8,128)S(1)} %bitcast.30), channel_id=1, source_target_pairs={{0,3},{1,2},{2,1},{3,0},{4,7},{5,6},{6,5},{7,4},{8,11},{9,10},{10,... | collective-permute-start | bytes 245768 | tf_op jit(solution)/shard_map/ppermute | solution.py:302
  72.9 9.7 %collective-permute-start.29 = (f32[16,1280]{1,0:T(8,128)S(1)}, f32[16,1280]{1,0:T(8,128)S(1)}, u32[]{:S(2)}, u32[]{:S(2)}) collective-permute-start(f32[16,1280]{1,0:T(8,128)S(1)} %bitcast.29), channel_id=1, source_target_pairs={{0,2},{1,3},{2,0},{3,1},{4,6},{5,7},{6,4},{7,5},{8,10},{9,11},{10,... | collective-permute-start | bytes 245768 | tf_op jit(solution)/shard_map/ppermute | solution.py:302
  72.9 9.7 %collective-permute-start.30 = (f32[16,1280]{1,0:T(8,128)S(1)}, f32[16,1280]{1,0:T(8,128)S(1)}, u32[]{:S(2)}, u32[]{:S(2)}) collective-permute-start(f32[16,1280]{1,0:T(8,128)S(1)} %bitcast.28), channel_id=1, source_target_pairs={{0,1},{1,0},{2,3},{3,2},{4,5},{5,4},{6,7},{7,6},{8,9},{9,8},{10,11... | collective-permute-start | bytes 245768 | tf_op jit(solution)/shard_map/ppermute | solution.py:302
  76.1 8.7 %collective-permute-start.14 = (f32[1,16,1280]{2,1,0:T(8,128)S(1)}, f32[1,16,1280]{2,1,0:T(8,128)S(1)}, u32[]{:S(2)}, u32[]{:S(2)}) collective-permute-start(f32[1,16,1280]{2,1,0:T(8,128)S(1)} %get-tuple-element.56), channel_id=1, source_target_pairs={{0,2},{1,3},{2,0},{3,1},{4,6},{5,7},{6,4},{7,5},{8,10},{9,11},{10,... | collective-permute-start | bytes 245768 | tf_op jit(solution)/shard_map/ppermute | solution.py:302
  (10 other events, 34.7 us)
